TPU v7x, 32 devices: a whole 2x2x4 slice. The times are simulated.
32 devices in a mesh: expert: 8 (over z, x), dp: 4 (over y, core).
Axes of the slice: x: 2, y: 2, z: 4, core: 2. Of those that a mesh axis runs over, the one named last changes fastest.
Arguments:
- layer_in: bfloat16 [4096, 1024], P(('expert', 'dp')), may hold values from -6 to 6
- routes: int32 [4096, 2], P(('expert', 'dp')), may hold values from 0 to 15, as said below
- queue_slots: int32 [4096, 2], P(('expert', 'dp')), may hold values from -1 to 4, as said below
- norm_attn: float32 [1024], replicated, may hold values from 0.5 to 1.5
- w_query: bfloat16 [1024, 1024], replicated, may hold values from -0.078125 to 0.078125
- w_key: bfloat16 [1024, 1024], replicated, may hold values from -0.078125 to 0.078125
- w_value: bfloat16 [1024, 1024], replicated, may hold values from -0.1875 to 0.1875
- w_out: bfloat16 [1024, 1024], replicated, may hold values from -0.75 to 0.75
- rel_table: float32 [32, 16], replicated, may hold values from -4 to 4
- norm_moe: float32 [1024], replicated, may hold values from 0.5 to 1.5
- router: float32 [1024, 16], replicated, may hold values from -0.375 to 0.375
- w_gate: bfloat16 [16, 1024, 2816], P('expert', None, 'dp'), may hold values from -0.1875 to 0.1875
- w_up: bfloat16 [16, 1024, 2816], P('expert', None, 'dp'), may hold values from -0.1875 to 0.1875
- w_down: bfloat16 [16, 2816, 1024], P('expert', 'dp'), may hold values from -0.109375 to 0.109375
- cotangent: bfloat16 [4096, 1024], P(('expert', 'dp')), may hold values from -6 to 6
Outputs:
- layer_out: bfloat16 [4096, 1024], P(('expert', 'dp'))
- grad_input: float32 [4096, 1024], P(('expert', 'dp'))
- grad_norm_attn: float32 [1024], replicated
- grad_w_query: float32 [1024, 1024], replicated
- grad_w_key: float32 [1024, 1024], replicated
- grad_w_value: float32 [1024, 1024], replicated
- grad_w_out: float32 [1024, 1024], replicated
- grad_rel_table: float32 [32, 16], replicated
- grad_norm_moe: float32 [1024], replicated
- grad_router: float32 [1024, 16], replicated
- grad_w_gate: float32 [16, 1024, 2816], P('expert', None, 'dp')
- grad_w_up: float32 [16, 1024, 2816], P('expert', None, 'dp')
- grad_w_down: float32 [16, 2816, 1024], P('expert', 'dp')
Inputs may be any that keep to these rules, and one draw needn't show every extreme that they name: `routes`: each token names two different experts. `queue_slots`: A choice's place in its expert's queue within its routing group of 32 consecutive tokens, where all first choices queue before all second choices; -1 where 5 places are already taken. Within a group each place of an expert is held by at most one choice, and an expert's places are taken from 0 upward without gaps.
All inputs are finite; a program needn't handle non-finite values.
Results may differ from a plain program's by a relative error of at most 0.014.
The roundings to bfloat16 on the way count: a program that leaves them out, or rounds other values in their place, can miss the bound.
Values may be sent and summed in bfloat16 or wider, within the bound.
A program may use at most 192 MiB of HBM per device.

v0:
```python
import jax
import jax.numpy as jnp
from jax import lax
from jax.sharding import PartitionSpec as P

MICRO = 4


epsilon = 1e-06
bucket_edges = (12, 16, 23, 32, 46, 64, 91)
highest = lax.Precision.HIGHEST


def rms_scale(values):
    return lax.rsqrt(jnp.mean(values * values, axis=-1, keepdims=True) + epsilon)


def bias_block(first_row, rows_count, seq_len, rel_table):
    query_pos = first_row + jnp.arange(rows_count, dtype=jnp.int32)
    key_pos = jnp.arange(seq_len, dtype=jnp.int32)
    relative = key_pos[None, :] - query_pos[:, None]
    distance = jnp.abs(relative)
    far_bucket = jnp.full_like(distance, 8)
    for threshold in bucket_edges:
        far_bucket = far_bucket + (distance >= threshold).astype(jnp.int32)
    bucketed = jnp.where(distance < 8, distance, far_bucket) + 16 * (relative > 0).astype(jnp.int32)
    bucket_ids = jnp.arange(rel_table.shape[0], dtype=jnp.int32)
    one_hot = (bucketed[None, :, :] == bucket_ids[:, None, None]).astype(jnp.float32)
    return (one_hot, jnp.einsum("bij,bh->hij", one_hot, rel_table, precision=highest))


def attend_block(offset, query_heads, key_heads, value_heads, rel_table, block_rows):
    seq_len = key_heads.shape[0]
    one_hot, bias = bias_block(offset, block_rows, seq_len, rel_table)
    scores = (
        jnp.einsum("ihd,jhd->hij", query_heads, key_heads, preferred_element_type=jnp.float32)
        + bias
    )
    row_max = jnp.max(scores, axis=-1, keepdims=True)
    exponent = jnp.exp(scores - row_max)
    totals = jnp.sum(exponent, axis=-1, keepdims=True)
    probs_low = (exponent / totals).astype(jnp.bfloat16)
    context = jnp.einsum(
        "hij,jhd->ihd", probs_low, value_heads, preferred_element_type=jnp.float32
    ).astype(jnp.bfloat16)
    return (context, row_max[..., 0] + jnp.log(totals[..., 0]))


def gated_product(gate_pre, up_pre):
    return jax.nn.gelu(gate_pre, approximate=True) * up_pre


def expert_forward(expert_rows, gate_w, up_w):
    gate_pre = jnp.einsum("rjd,jdf->rjf", expert_rows, gate_w, preferred_element_type=jnp.float32)
    up_pre = jnp.einsum("rjd,jdf->rjf", expert_rows, up_w, preferred_element_type=jnp.float32)
    hidden = gated_product(gate_pre, up_pre).astype(jnp.bfloat16)
    return (gate_pre, up_pre, hidden)


def expert_backward(expert_rows, gate_pre, up_pre, hidden, grad_rows, gate_w, up_w, down_w):
    hidden_grad = jnp.einsum("rjd,jfd->rjf", grad_rows, down_w, preferred_element_type=jnp.float32)
    grad_down = jnp.einsum("rjf,rjd->jfd", hidden, grad_rows, preferred_element_type=jnp.float32)
    product_value, pullback = jax.vjp(gated_product, gate_pre, up_pre)
    gate_grad, up_grad = pullback(hidden_grad)
    gate_grad = gate_grad.astype(jnp.bfloat16)
    up_grad = up_grad.astype(jnp.bfloat16)
    grad_gate = jnp.einsum(
        "rjd,rjf->jdf", expert_rows, gate_grad, preferred_element_type=jnp.float32
    )
    grad_up = jnp.einsum("rjd,rjf->jdf", expert_rows, up_grad, preferred_element_type=jnp.float32)
    rows_grad = jnp.einsum("rjf,jdf->rjd", gate_grad, gate_w, preferred_element_type=jnp.float32)
    rows_grad = rows_grad + jnp.einsum(
        "rjf,jdf->rjd", up_grad, up_w, preferred_element_type=jnp.float32
    )
    return (rows_grad, grad_gate, grad_up, grad_down)


def spread_to_holders(buffer, holders, expert_groups, per_device):
    micro_count, capacity, expert_count, model_width = buffer.shape
    grouped = buffer.reshape(micro_count, capacity, expert_groups, 1, per_device, model_width)
    spread = jnp.broadcast_to(
        grouped, (micro_count, capacity, expert_groups, holders, per_device, model_width)
    )
    return spread.reshape(micro_count, capacity, expert_groups * holders * per_device, model_width)


def shards(
    layer_in,
    routes,
    queue_slots,
    norm_attn,
    w_query,
    w_key,
    w_value,
    w_out,
    rel_table,
    norm_moe,
    router,
    w_gate,
    w_up,
    w_down,
    cotangent,
):
    seq_len, model_width = layer_in.shape
    head_count = rel_table.shape[1]
    head_size = w_query.shape[1] // head_count
    expert_count = router.shape[1]
    per_device = w_gate.shape[0]
    expert_groups = lax.axis_size("expert")
    holders = lax.axis_size("dp")
    group_len = seq_len // MICRO
    capacity = (5 * group_len + 2 * expert_count - 1) // (2 * expert_count)
    block_rows = min(512, seq_len)
    block_count = seq_len // block_rows
    offsets = jnp.arange(block_count, dtype=jnp.int32) * block_rows
    split_heads = (seq_len, head_count, head_size)
    layer_rows = layer_in.astype(jnp.float32)
    inv_attn = rms_scale(layer_rows)
    normed_attn = layer_rows * inv_attn
    attn_in = (normed_attn * norm_attn).astype(jnp.bfloat16)
    queries = jnp.dot(attn_in, w_query, preferred_element_type=jnp.float32).astype(jnp.bfloat16)
    key_rows = jnp.dot(attn_in, w_key, preferred_element_type=jnp.float32).astype(jnp.bfloat16)
    value_rows = jnp.dot(attn_in, w_value, preferred_element_type=jnp.float32).astype(jnp.bfloat16)
    query_heads = queries.reshape(split_heads)
    key_heads = key_rows.reshape(split_heads)
    value_heads = value_rows.reshape(split_heads)

    def attend(offset):
        return attend_block(offset, query_heads, key_heads, value_heads, rel_table, block_rows)

    context_blocks, lse_blocks = lax.map(attend, offsets)
    context = context_blocks.reshape(seq_len, model_width)
    attn = jnp.dot(context, w_out, preferred_element_type=jnp.float32)
    residual = layer_rows + attn
    inv_moe = rms_scale(residual)
    normed_moe = residual * inv_moe
    moe_in = normed_moe * norm_moe
    logits = jnp.dot(moe_in, router, precision=highest)
    gate_prob = jax.nn.softmax(logits, axis=-1)
    expert_ids = jnp.arange(expert_count, dtype=jnp.int32)
    first_hot = (routes[:, 0:1] == expert_ids).astype(jnp.float32)
    second_hot = (routes[:, 1:2] == expert_ids).astype(jnp.float32)
    prob_first = jnp.sum(gate_prob * first_hot, axis=-1, keepdims=True)
    prob_second = jnp.sum(gate_prob * second_hot, axis=-1, keepdims=True)
    weight_first = prob_first / (prob_first + prob_second)
    weight_second = prob_second / (prob_first + prob_second)
    slot_ids = jnp.arange(capacity * expert_count, dtype=jnp.int32)
    place = queue_slots * expert_count + routes
    kept = queue_slots >= 0
    slot_shape = (MICRO, group_len, capacity * expert_count)
    select_first = (
        ((place[:, 0:1] == slot_ids) & kept[:, 0:1]).astype(jnp.bfloat16).reshape(slot_shape)
    )
    select_second = (
        ((place[:, 1:2] == slot_ids) & kept[:, 1:2]).astype(jnp.bfloat16).reshape(slot_shape)
    )
    select_both = select_first + select_second
    moe_low = moe_in.astype(jnp.bfloat16).reshape(MICRO, group_len, model_width)
    dispatched = jnp.einsum(
        "gtp,gtd->gpd", select_both, moe_low, preferred_element_type=jnp.float32
    )
    dispatched = dispatched.astype(jnp.bfloat16).reshape(MICRO, capacity, expert_count, model_width)
    spread = spread_to_holders(dispatched, holders, expert_groups, per_device)
    received = lax.all_to_all(spread, ("expert", "dp"), split_axis=2, concat_axis=0, tiled=True)
    expert_rows = received.reshape(-1, per_device, model_width)
    gate_w, up_w, down_w = (w_gate, w_up, w_down)
    gate_pre, up_pre, hidden = expert_forward(expert_rows, gate_w, up_w)
    partial_out = jnp.einsum("rjf,jfd->rjd", hidden, down_w, preferred_element_type=jnp.float32)
    partial_out = partial_out.reshape(
        expert_groups * holders * MICRO, capacity, per_device, model_width
    )
    returned_out = lax.all_to_all(
        partial_out.astype(jnp.bfloat16), ("expert", "dp"), split_axis=0, concat_axis=2, tiled=True
    ).astype(partial_out.dtype)
    returned_out = returned_out.reshape(
        MICRO, capacity, expert_groups, holders, per_device, model_width
    )
    expert_out = (
        jnp.sum(returned_out, axis=3)
        .astype(jnp.bfloat16)
        .reshape(MICRO, capacity * expert_count, model_width)
    )
    picked_first = jnp.einsum(
        "gtp,gpd->gtd", select_first, expert_out, preferred_element_type=jnp.float32
    ).reshape(seq_len, model_width)
    picked_second = jnp.einsum(
        "gtp,gpd->gtd", select_second, expert_out, preferred_element_type=jnp.float32
    ).reshape(seq_len, model_width)
    moe = weight_first * picked_first + weight_second * picked_second
    layer_out = (residual + moe).astype(jnp.bfloat16)
    cot_rows = cotangent.astype(jnp.float32)
    grad_weight_first = jnp.sum(cot_rows * picked_first, axis=-1, keepdims=True)
    grad_weight_second = jnp.sum(cot_rows * picked_second, axis=-1, keepdims=True)
    sent_first = (
        (weight_first * cot_rows).astype(jnp.bfloat16).reshape(MICRO, group_len, model_width)
    )
    sent_second = (
        (weight_second * cot_rows).astype(jnp.bfloat16).reshape(MICRO, group_len, model_width)
    )
    grad_expert_out = jnp.einsum(
        "gtp,gtd->gpd", select_first, sent_first, preferred_element_type=jnp.float32
    )
    grad_expert_out = grad_expert_out + jnp.einsum(
        "gtp,gtd->gpd", select_second, sent_second, preferred_element_type=jnp.float32
    )
    grad_expert_out = grad_expert_out.astype(jnp.bfloat16).reshape(
        MICRO, capacity, expert_count, model_width
    )
    grad_spread = spread_to_holders(grad_expert_out, holders, expert_groups, per_device)
    grad_received = lax.all_to_all(
        grad_spread, ("expert", "dp"), split_axis=2, concat_axis=0, tiled=True
    )
    grad_rows = grad_received.reshape(-1, per_device, model_width)
    rows_grad, grad_w_gate, grad_w_up, grad_w_down = expert_backward(
        expert_rows, gate_pre, up_pre, hidden, grad_rows, gate_w, up_w, down_w
    )
    rows_grad = rows_grad.reshape(
        expert_groups * holders * MICRO, capacity, per_device, model_width
    )
    grad_returned = lax.all_to_all(
        rows_grad.astype(jnp.bfloat16), ("expert", "dp"), split_axis=0, concat_axis=2, tiled=True
    ).astype(rows_grad.dtype)
    grad_returned = grad_returned.reshape(
        MICRO, capacity, expert_groups, holders, per_device, model_width
    )
    grad_dispatched = (
        jnp.sum(grad_returned, axis=3)
        .astype(jnp.bfloat16)
        .reshape(MICRO, capacity * expert_count, model_width)
    )
    grad_from_slots = jnp.einsum(
        "gtp,gpd->gtd", select_both, grad_dispatched, preferred_element_type=jnp.float32
    )
    grad_from_slots = grad_from_slots.reshape(seq_len, model_width)
    mean_grad = weight_first * grad_weight_first + weight_second * grad_weight_second
    logit_first = weight_first * (grad_weight_first - mean_grad)
    logit_second = weight_second * (grad_weight_second - mean_grad)
    grad_logits = logit_first * first_hot + logit_second * second_hot
    grad_router = jnp.einsum("sd,se->de", moe_in, grad_logits, precision=highest)
    grad_moe_in = grad_from_slots + jnp.einsum("se,de->sd", grad_logits, router, precision=highest)
    grad_norm_moe = jnp.sum(grad_moe_in * normed_moe, axis=0)
    grad_normed = grad_moe_in * norm_moe
    grad_residual = cot_rows + inv_moe * (
        grad_normed - normed_moe * jnp.mean(grad_normed * normed_moe, axis=-1, keepdims=True)
    )
    grad_attn_low = grad_residual.astype(jnp.bfloat16)
    grad_w_out = jnp.einsum("se,sd->ed", context, grad_attn_low, preferred_element_type=jnp.float32)
    grad_context = jnp.einsum(
        "sd,ed->se", grad_attn_low, w_out, preferred_element_type=jnp.float32
    ).astype(jnp.bfloat16)
    grad_context_heads = grad_context.reshape(split_heads)

    def attend_back(totals, block_in):
        grad_keys_acc, grad_values_acc, grad_table = totals
        offset, lse_block = block_in
        one_hot, bias = bias_block(offset, block_rows, seq_len, rel_table)
        scores = (
            jnp.einsum("ihd,jhd->hij", query_heads, key_heads, preferred_element_type=jnp.float32)
            + bias
        )
        attn_probs = jnp.exp(scores - lse_block[:, :, None])
        probs_low = attn_probs.astype(jnp.bfloat16)
        grad_values_acc = grad_values_acc + jnp.einsum(
            "hij,ihd->jhd", probs_low, grad_context_heads, preferred_element_type=jnp.float32
        )
        grad_probs = jnp.einsum(
            "ihd,jhd->hij", grad_context_heads, value_heads, preferred_element_type=jnp.float32
        )
        grad_scores = attn_probs * (
            grad_probs - jnp.sum(attn_probs * grad_probs, axis=-1, keepdims=True)
        )
        grad_table = grad_table + jnp.einsum("bij,hij->bh", one_hot, grad_scores, precision=highest)
        scores_low = grad_scores.astype(jnp.bfloat16)
        grad_query_blk = jnp.einsum(
            "hij,jhd->ihd", scores_low, key_heads, preferred_element_type=jnp.float32
        ).astype(jnp.bfloat16)
        grad_keys_acc = grad_keys_acc + jnp.einsum(
            "hij,ihd->jhd", scores_low, query_heads, preferred_element_type=jnp.float32
        )
        return ((grad_keys_acc, grad_values_acc, grad_table), grad_query_blk)

    start_totals = (
        jnp.zeros(split_heads, jnp.float32),
        jnp.zeros(split_heads, jnp.float32),
        jnp.zeros(rel_table.shape, jnp.float32),
    )
    end_totals, grad_query_blocks = lax.scan(attend_back, start_totals, (offsets, lse_blocks))
    grad_keys_acc, grad_values_acc, grad_rel_table = end_totals
    grad_queries = grad_query_blocks.reshape(seq_len, model_width)
    grad_keys = grad_keys_acc.reshape(seq_len, model_width).astype(jnp.bfloat16)
    grad_values = grad_values_acc.reshape(seq_len, model_width).astype(jnp.bfloat16)
    grad_w_query = jnp.einsum(
        "sd,se->de", attn_in, grad_queries, preferred_element_type=jnp.float32
    )
    grad_w_key = jnp.einsum("sd,se->de", attn_in, grad_keys, preferred_element_type=jnp.float32)
    grad_w_value = jnp.einsum("sd,se->de", attn_in, grad_values, preferred_element_type=jnp.float32)
    grad_attn_in = jnp.einsum(
        "se,de->sd", grad_queries, w_query, preferred_element_type=jnp.float32
    )
    grad_attn_in = grad_attn_in + jnp.einsum(
        "se,de->sd", grad_keys, w_key, preferred_element_type=jnp.float32
    )
    grad_attn_in = grad_attn_in + jnp.einsum(
        "se,de->sd", grad_values, w_value, preferred_element_type=jnp.float32
    )
    grad_norm_attn = jnp.sum(grad_attn_in * normed_attn, axis=0)
    grad_normed_attn = grad_attn_in * norm_attn
    grad_input = grad_residual + inv_attn * (
        grad_normed_attn
        - normed_attn * jnp.mean(grad_normed_attn * normed_attn, axis=-1, keepdims=True)
    )
    summed = lax.psum(
        (
            grad_norm_attn,
            grad_w_query,
            grad_w_key,
            grad_w_value,
            grad_w_out,
            grad_rel_table,
            grad_norm_moe,
            grad_router,
        ),
        ("expert", "dp"),
    )
    return (
        layer_out,
        grad_input,
        summed[0],
        summed[1],
        summed[2],
        summed[3],
        summed[4],
        summed[5],
        summed[6],
        summed[7],
        grad_w_gate,
        grad_w_up,
        grad_w_down,
    )


def solution(mesh):
    in_specs = (
        P(("expert", "dp"), None),
        P(("expert", "dp"), None),
        P(("expert", "dp"), None),
        P(),
        P(),
        P(),
        P(),
        P(),
        P(),
        P(),
        P(),
        P("expert", None, "dp"),
        P("expert", None, "dp"),
        P("expert", "dp", None),
        P(("expert", "dp"), None),
    )
    out_specs = (
        P(("expert", "dp"), None),
        P(("expert", "dp"), None),
        P(),
        P(),
        P(),
        P(),
        P(),
        P(),
        P(),
        P(),
        P("expert", None, "dp"),
        P("expert", None, "dp"),
        P("expert", "dp", None),
    )
    return jax.shard_map(shards, mesh=mesh, in_specs=in_specs, out_specs=out_specs, check_vma=False)
```

profile of v0, /device:TPU:1, one launch (start us, length us, event | category | flops | bytes accessed | tf_op | source)
XLA Modules:
  0.0 683.1 jit_solution(15179382950645383366)
XLA Ops:
  13.4 2.5 copy.91
  15.9 2.8 convolution_convert_fusion.7
  19.8 2.8 convolution_convert_fusion.6
  32.6 2.6 broadcast_in_dim.46
  38.1 67.0 %all_to_all.48 = bf16[4,5,64,1024]{3,0,1,2:T(4,128)(2,1)S(1)} all-to-all(bf16[4,5,64,1024]{3,0,1,2:T(4,128)(2,1)S(1)} %bitcast.150), channel_id=1, replica_groups=mesh['expert'=8,'dp'=4] {'expert','dp'}, dimensions={2} | all-to-all | bytes 5242880 | tf_op jit(solution)/shard_map/all_to_all | solution.py:164
  105.2 2.6 copy.95
  107.8 2.5 fusion.24
  110.6 4.9 fusion.8
  119.0 4.6 copy.98
  123.6 3.8 all-to-all-start.1
  131.0 56.2 %all-to-all-done.1 = bf16[128,5,2,1024]{3,2,1,0:T(2,128)(2,1)} async-done(((bf16[128,5,2,1024]{3,2,1,0:T(2,128)(2,1)}), bf16[128,5,2,1024]{3,2,1,0:T(2,128)(2,1)}, u32[]{:S(2)}, u32[]{:S(2)}) %all-to-all-start.1) | async-done | bytes 2621472 | tf_op jit(solution)/shard_map/all_to_all | solution.py:172
  187.3 6.2 reduce
  200.6 2.6 broadcast_in_dim.48
  206.1 65.0 %all_to_all.49 = bf16[4,5,64,1024]{3,0,1,2:T(4,128)(2,1)S(1)} all-to-all(bf16[4,5,64,1024]{3,0,1,2:T(4,128)(2,1)S(1)} %bitcast.152), channel_id=1, replica_groups=mesh['expert'=8,'dp'=4] {'expert','dp'}, dimensions={2} | all-to-all | bytes 5242880 | tf_op jit(solution)/shard_map/all_to_all | solution.py:210
  271.1 2.6 copy.104
  273.7 5.0 fusion.7
  284.2 4.2 copy.106
  288.4 3.8 all-to-all-start.3
  293.8 58.3 %all-to-all-done.3 = bf16[128,5,2,1024]{3,2,1,0:T(2,128)(2,1)} async-done(((bf16[128,5,2,1024]{3,2,1,0:T(2,128)(2,1)}), bf16[128,5,2,1024]{3,2,1,0:T(2,128)(2,1)}, u32[]{:S(2)}, u32[]{:S(2)}) %all-to-all-start.3) | async-done | bytes 2621472 | tf_op jit(solution)/shard_map/all_to_all | solution.py:220
  352.1 5.4 reduce.1
  364.2 2.7 fusion.70
  367.0 2.8 fusion.122
  369.8 2.8 fusion.120
  372.6 2.8 fusion.118
  375.5 8.1 %fusion.18 = f32[2,1024,704]{1,2,0:T(8,128)} fusion(bf16[640,2,704]{0,2,1:T(8,128)(2,1)} %copy-done.88, bf16[640,2,1024]{2,1,0:T(2,128)(2,1)} %bitcast.158), kind=kOutput, calls=%fused_computation.28 | convolution fusion | flops 1845493760 | bytes 10190848 | tf_op jit(solution)/shard_map/rjd,rjf->jdf/dot_general | solution.py:67
  383.6 5.0 fusion.20
  388.6 5.0 fusion.12
  395.0 2.6 fusion.27
  397.6 2.6 fusion.130
  402.1 40.5 %all-reduce = (f32[1024]{0:T(1024)}, f32[32,16]{0,1:T(8,128)}, f32[1024]{0:T(1024)}) all-reduce(f32[1024]{0:T(1024)S(1)} %get-tuple-element.58, f32[32,16]{0,1:T(8,128)S(1)} %fusion.27, f32[1024]{0:T(1024)S(1)} %copy-done.50), channel_id=1, replica_groups=mesh['expert'=8,'dp'=4] {'expert','dp'}, use_global_device_ids=true, to_apply=%region_16.17 | all-reduce | flops 2560 | bytes 20480 | tf_op jit(solution)/shard_map/psum | solution.py:312
  443.7 217.1 %all-reduce.4.cloned.1.call-done = (f32[1024,1024]{1,0:T(8,128)}, f32[1024,1024]{1,0:T(8,128)}, f32[1024,1024]{1,0:T(8,128)}, f32[1024,1024]{1,0:T(8,128)}, f32[1024,16]{0,1:T(8,128)}) async-done(((f32[1024,1024]{1,0:T(8,128)}, f32[1024,1024]{1,0:T(8,128)}, f32[1024,1024]{1,0:T(8,128)}, f32[1024,1024]{1,0:T(8,128)}, f32[1024,16]{0,1:T(8,128)}), (f32[1024,1024]{1,0:T(8,128)}, f32[1024,1024]{1,0:T(8,128)}, ...) | async-done | bytes 16842768 | tf_op jit(solution)/shard_map/psum | solution.py:312
  660.8 4.9 copy.150
  (252 shorter events, 65.0 us)
Async XLA Ops:
  7.2 109.5 %copy-start = (bf16[2,704,1024]{2,1,0:T(8,128)(2,1)S(1)}, bf16[2,704,1024]{2,1,0:T(8,128)(2,1)}, u32[]{:S(2)}) copy-start(bf16[2,704,1024]{2,1,0:T(8,128)(2,1)} %param.28) | copy-start | bytes 8650756
  8.5 11.3 %copy-start.48 = (f32[128]{0:T(128)}, f32[128]{0:T(128)S(1)}, u32[]{:S(2)}) copy-start(f32[128]{0:T(128)S(1)} %add_rsqrt_fusion.1) | copy-start | bytes 1540
  8.5 7.4 %copy-start.4 = (bf16[128,1024]{1,0:T(8,128)(2,1)S(1)}, bf16[128,1024]{1,0:T(8,128)(2,1)}, u32[]{:S(2)}) copy-start(bf16[128,1024]{1,0:T(8,128)(2,1)} %param.15) | copy-start | bytes 786436
  8.5 7.4 %copy-start.35 = (f32[1024]{0:T(1024)S(1)}, f32[1024]{0:T(1024)}, u32[]{:S(2)}) copy-start(f32[1024]{0:T(1024)} %param.18) | copy-start | bytes 12292
  29.5 8.6 %copy-start.51 = (f32[128]{0:T(128)}, f32[128]{0:T(128)S(1)}, u32[]{:S(2)}) copy-start(f32[128]{0:T(128)S(1)} %add_rsqrt_fusion) | copy-start | bytes 1540
  29.7 8.4 %copy-start.43 = (s32[4,32]{1,0:T(4,128)}, s32[4,32]{1,0:T(4,128)S(1)}, u32[]{:S(2)}) copy-start(s32[4,32]{1,0:T(4,128)S(1)} %eq.119) | copy-start | bytes 1540
  29.8 8.3 %copy-start.40 = (s32[4,32]{1,0:T(4,128)}, s32[4,32]{1,0:T(4,128)S(1)}, u32[]{:S(2)}) copy-start(s32[4,32]{1,0:T(4,128)S(1)} %eq.115) | copy-start | bytes 1540
  29.9 8.2 %copy-start.62 = (pred[4,32]{1,0:T(4,128)(4,1)}, pred[4,32]{1,0:T(4,128)(4,1)S(1)}, u32[]{:S(2)}) copy-start(pred[4,32]{1,0:T(4,128)(4,1)S(1)} %and.27) | copy-start | bytes 388
  30.0 8.2 %copy-start.55 = (pred[4,32]{1,0:T(4,128)(4,1)}, pred[4,32]{1,0:T(4,128)(4,1)S(1)}, u32[]{:S(2)}) copy-start(pred[4,32]{1,0:T(4,128)(4,1)S(1)} %and.24) | copy-start | bytes 388
  110.6 4.9 copy-start.89
  123.6 63.7 %all-to-all-start.1 = ((bf16[128,5,2,1024]{3,2,1,0:T(2,128)(2,1)}), bf16[128,5,2,1024]{3,2,1,0:T(2,128)(2,1)}, u32[]{:S(2)}, u32[]{:S(2)}) async-start(bf16[128,5,2,1024]{3,2,1,0:T(2,128)(2,1)} %bitcast.148), calls=%async_computation.1 | async-start | bytes 5242880 | tf_op jit(solution)/shard_map/all_to_all | solution.py:172
  187.3 8.9 %copy-start.44 = (s32[4,32]{1,0:T(4,128)S(1)}, s32[4,32]{1,0:T(4,128)}, u32[]{:S(2)}) copy-start(s32[4,32]{1,0:T(4,128)} %copy-done.43) | copy-start | bytes 1540
  193.5 5.2 copy-start.41
  193.5 5.2 copy-start.56
  206.1 67.6 %copy-start.91 = (f32[2,640,704]{1,2,0:T(8,128)S(1)}, f32[2,640,704]{1,2,0:T(8,128)}, u32[]{:S(2)}) copy-start(f32[2,640,704]{1,2,0:T(8,128)} %get-tuple-element.103) | copy-start | bytes 10813444
  273.7 5.0 copy-start.19
  273.7 5.0 copy-start.81
  288.4 63.7 %all-to-all-start.3 = ((bf16[128,5,2,1024]{3,2,1,0:T(2,128)(2,1)}), bf16[128,5,2,1024]{3,2,1,0:T(2,128)(2,1)}, u32[]{:S(2)}, u32[]{:S(2)}) async-start(bf16[128,5,2,1024]{3,2,1,0:T(2,128)(2,1)} %bitcast.149), calls=%async_computation.3 | async-start | bytes 5242880 | tf_op jit(solution)/shard_map/all_to_all | solution.py:220
  292.3 65.6 %copy-start.42 = (s32[4,32]{1,0:T(4,128)S(1)}, s32[4,32]{1,0:T(4,128)}, u32[]{:S(2)}) copy-start(s32[4,32]{1,0:T(4,128)} %copy-done.40) | copy-start | bytes 1540
  292.3 65.6 %copy-start.45 = (s32[4,32]{1,0:T(4,128)S(1)}, s32[4,32]{1,0:T(4,128)}, u32[]{:S(2)}) copy-start(s32[4,32]{1,0:T(4,128)} %copy-done.43) | copy-start | bytes 1540
  292.3 65.6 %copy-start.57 = (pred[4,32]{1,0:T(4,128)(4,1)S(1)}, pred[4,32]{1,0:T(4,128)(4,1)}, u32[]{:S(2)}) copy-start(pred[4,32]{1,0:T(4,128)(4,1)} %copy-done.55) | copy-start | bytes 388
  292.3 65.6 %copy-start.64 = (pred[4,32]{1,0:T(4,128)(4,1)S(1)}, pred[4,32]{1,0:T(4,128)(4,1)}, u32[]{:S(2)}) copy-start(pred[4,32]{1,0:T(4,128)(4,1)} %copy-done.62) | copy-start | bytes 388
  292.3 368.5 %all-reduce.4.cloned.1.call-start = ((), (), s32[]{:S(2)}) async-start(), calls=%async_computation.4 | async-start | bytes 33685504 | tf_op jit(solution)/shard_map/psum | solution.py:312
  363.7 6.0 copy-start.26
  375.4 8.2 %copy-start.18 = (bf16[32,4,5,2,1024]{4,3,2,1,0:T(2,128)(2,1)S(1)}, bf16[32,4,5,2,1024]{4,3,2,1,0:T(2,128)(2,1)}, u32[]{:S(2)}) copy-start(bf16[32,4,5,2,1024]{4,3,2,1,0:T(2,128)(2,1)} %copy-done.17) | copy-start | bytes 7864324
  375.5 8.2 %copy-start.87 = (bf16[640,2,704]{0,2,1:T(8,128)(2,1)S(1)}, bf16[640,2,704]{0,2,1:T(8,128)(2,1)}, u32[]{:S(2)}) copy-start(bf16[640,2,704]{0,2,1:T(8,128)(2,1)} %copy-done.86) | copy-start | bytes 5406724
  383.6 5.0 copy-start.20
  383.6 5.0 copy-start.85
  395.0 5.2 copy-start.8
  395.0 5.2 copy-start.27
  660.8 4.9 copy-start.16
  669.4 6.4 copy-start.1
  (63 other events, 173.8 us)
Sparse Core Ops, SparseCore 0:
  375.6 285.1 all-reduce.3
where the time goes:
time: 690 us; the launch traced here: 683 us
  waiting for transfers between devices  332 us (48%)
  blocking collectives  173 us (25%)
  matrix products  80.9 us (12%)
  local copies, waits for them, and re-layouts  56.4 us (8%)
  other arithmetic  18 us (3%)
  between operations  15.7 us (2%)
  starting transfers between devices  7.89 us (1%)
    psum x1, waiting for transfers between devices, shards(): lax.psum((grad_norm_attn, grad_w_query, grad_w_key, grad_w_value, grad_w_...  217 us
    all_to_all x1, blocking collectives, shards(): lax.all_to_all(spread, ('expert', 'dp'), split_axis=2, concat_axis=0, til...  67 us
    all_to_all x1, blocking collectives, shards(): lax.all_to_all(grad_spread, ('expert', 'dp'), split_axis=2, concat_axis=0...  65 us
    all_to_all x1, waiting for transfers between devices, shards(): lax.all_to_all(rows_grad.astype(jnp.bfloat16), ('expert', 'dp'), split_ax...  58.3 us
    all_to_all x1, waiting for transfers between devices, shards(): lax.all_to_all(partial_out.astype(jnp.bfloat16), ('expert', 'dp'), split_...  56.2 us
    psum x1, blocking collectives, shards(): lax.psum((grad_norm_attn, grad_w_query, grad_w_key, grad_w_value, grad_w_...  40.5 us
    unnamed x189, local copies, waits for them, and re-layouts  20.6 us
  transfers between devices with their start and end apart: 3, of which 3 were waited for; matrix products, arithmetic and copies ran while one was open for 5% of the time, Pallas kernels for 0%

commit v1 on v0

v1 whole, which is shorter than its diff:
```python
import functools
import math

import jax
import jax.numpy as jnp
from jax import lax
from jax.experimental import pallas as pl
from jax.experimental.pallas import tpu as pltpu
from jax.sharding import PartitionSpec as P

MICRO = 4

epsilon = 1e-06
bucket_edges = (12, 16, 23, 32, 46, 64, 91)
highest = lax.Precision.HIGHEST

MESH = pl.DeviceIdType.MESH
VMEM = pl.BlockSpec(memory_space=pltpu.VMEM)
DMA = pltpu.SemaphoreType.DMA


class Place:
    def __init__(self, n_expert, n_dp):
        self.n_expert, self.n_dp = n_expert, n_dp
        self.nz = math.gcd(n_expert, 4)
        self.nx = n_expert // self.nz
        self.ny = n_dp // 2
        self.e = lax.axis_index("expert")
        self.d = lax.axis_index("dp")
        self.z, self.x = self.e // self.nx, self.e % self.nx
        self.y, self.c = self.d // 2, self.d % 2

    def at(self, z=None, x=None, y=None, c=None, e=None):
        z = self.z if z is None else z
        x = self.x if x is None else x
        y = self.y if y is None else y
        c = self.c if c is None else c
        e = z * self.nx + x if e is None else e
        return (e, y * 2 + c)


def remote(src, dst, send, recv, device):
    copy = pltpu.make_async_remote_copy(
        src_ref=src, dst_ref=dst, send_sem=send, recv_sem=recv, device_id=device, device_id_type=MESH
    )
    copy.start()
    return copy


def greet(devices):
    barrier = pltpu.get_barrier_semaphore()
    for device in devices:
        pl.semaphore_signal(barrier, inc=1, device_id=device, device_id_type=MESH)
    pl.semaphore_wait(barrier, len(devices))


def column_peers(me):
    out = [me.at(c=1 - me.c)]
    out += [me.at(y=(me.y + k) % me.ny) for k in range(1, me.ny)]
    out += [me.at(e=(me.e + k) % me.n_expert) for k in range(1, me.n_expert)]
    return out


def send_rows(me, rows, recv, send_sem, recv_sem):
    copies = []
    for k in range(1, me.n_expert):
        to = (me.e + k) % me.n_expert
        copies.append(
            remote(rows.at[to], recv.at[me.c, me.y, me.e], send_sem.at[k], recv_sem.at[k], me.at(e=to))
        )
    recv[me.c, me.y, me.e] = rows[me.e]
    return copies


def pass_on(me, recv, came, sy, ry, sc, rc):
    along_y = []
    for k in range(me.n_expert):
        src = (me.e - k + me.n_expert) % me.n_expert
        if k:
            came[k - 1].wait_recv()
        block = recv.at[me.c, me.y, src]
        for s in range(1, me.ny):
            along_y.append(
                remote(block, block, sy.at[s - 1, k], ry.at[s - 1, k], me.at(y=(me.y + s) % me.ny))
            )
    block = recv.at[me.c, me.y]
    across = [remote(block, block, sc.at[0], rc.at[0], me.at(c=1 - me.c))]
    return along_y, across


def pass_across(me, recv, along_y, across, sc, rc):
    for copy in along_y:
        copy.wait_recv()
    for s in range(1, me.ny):
        block = recv.at[me.c, (me.y - s + me.ny) % me.ny]
        across.append(remote(block, block, sc.at[s], rc.at[s], me.at(c=1 - me.c)))


def spread_kernel(
    sizes, rows_per, info_ref, cot_ref, moe_ref, w_ref, g_out, x_out, w_out,
    info_all, tok, wext, rows_g, rows_x, rows_w, sem_tok_s, sem_tok_r, se, re, sy, ry, sc, rc,
):
    me = Place(*sizes)
    micro, cap, per_core = rows_per
    seq = cot_ref.shape[0]
    greet(column_peers(me))
    mate = me.at(c=1 - me.c)
    c = me.c
    first = []
    info_all[c] = info_ref[...]
    tok[0, c] = cot_ref[...]
    tok[1, c] = moe_ref[...]
    lanes = lax.broadcasted_iota(jnp.int32, (seq, 128), 1)
    for k in range(2):
        w = w_ref[:, k : k + 1]
        hi = w.astype(jnp.bfloat16).astype(jnp.float32)
        mid = (w - hi).astype(jnp.bfloat16).astype(jnp.float32)
        low = w - hi - mid
        wext[c, k] = jnp.where(
            lanes == 0, hi, jnp.where(lanes == 1, mid, jnp.where(lanes == 2, low, 0.0))
        ).astype(jnp.bfloat16)
    first.append(remote(info_all.at[c], info_all.at[c], sem_tok_s.at[0], sem_tok_r.at[0], mate))
    first.append(remote(tok.at[0, c], tok.at[0, c], sem_tok_s.at[1], sem_tok_r.at[1], mate))
    first.append(remote(tok.at[1, c], tok.at[1, c], sem_tok_s.at[2], sem_tok_r.at[2], mate))
    first.append(remote(wext.at[c], wext.at[c], sem_tok_s.at[3], sem_tok_r.at[3], mate))
    first[0].wait_recv()
    n_rows = me.n_expert * 2 * per_core
    row_ids = lax.broadcasted_iota(jnp.int32, (n_rows, seq), 0)
    group = lax.broadcasted_iota(jnp.int32, (1, seq), 1) // (seq // micro)
    hots = [[], []]
    for cc in range(2):
        for k in range(2):
            route = info_all[cc, k : k + 1, :]
            slot = info_all[cc, 2 + k : 3 + k, :]
            target = (route // 2) * (2 * per_core) + cc * per_core + group * cap + slot
            target = jnp.where((slot >= 0) & (route % 2 == c), target, -1)
            hots[k].append(jnp.where(row_ids == target, 1.0, 0.0))
    hot1 = [h.astype(jnp.bfloat16) for h in hots[0]]
    hot2 = [h.astype(jnp.bfloat16) for h in hots[1]]
    both = [(p + q).astype(jnp.bfloat16) for p, q in zip(*hots)]

    def gather(left, right):
        total = None
        for p, q in zip(left, right):
            term = jnp.dot(p, q, preferred_element_type=jnp.float32)
            total = term if total is None else total + term
        return total.astype(jnp.bfloat16).reshape(me.n_expert, 2 * per_core, -1)

    first[1].wait_recv()
    rows_g[...] = gather(both, [tok[0, 0], tok[0, 1]])
    came_g = send_rows(me, rows_g, g_out, se.at[0], re.at[0])
    first[2].wait_recv()
    first[3].wait_recv()
    rows_x[...] = gather(both, [tok[1, 0], tok[1, 1]])
    came_x = send_rows(me, rows_x, x_out, se.at[1], re.at[1])
    rows_w[...] = gather(hot1 + hot2, [wext[0, 0], wext[1, 0], wext[0, 1], wext[1, 1]])
    came_w = send_rows(me, rows_w, w_out, se.at[2], re.at[2])
    state = []
    for i, (ref, came) in enumerate(((g_out, came_g), (x_out, came_x), (w_out, came_w))):
        state.append(pass_on(me, ref, came, sy.at[i], ry.at[i], sc.at[i], rc.at[i]))
    for i, ref in enumerate((g_out, x_out, w_out)):
        pass_across(me, ref, state[i][0], state[i][1], sc.at[i], rc.at[i])
    for along_y, across in state:
        for copy in across:
            copy.wait()
        for copy in along_y:
            copy.wait_send()
    for copy in first + came_g + came_x + came_w:
        copy.wait_send()


def spread(sizes, micro, cap, info, cot, moe, weights):
    n_expert, n_dp = sizes
    ny, per_core = n_dp // 2, micro * cap
    seq, width = cot.shape
    block = (2, ny, n_expert, 2 * per_core)
    bf = jnp.bfloat16
    return pl.pallas_call(
        functools.partial(spread_kernel, sizes, (micro, cap, per_core)),
        out_shape=(
            jax.ShapeDtypeStruct(block + (width,), bf),
            jax.ShapeDtypeStruct(block + (width,), bf),
            jax.ShapeDtypeStruct(block + (128,), bf),
        ),
        in_specs=[VMEM] * 4,
        out_specs=(VMEM,) * 3,
        scratch_shapes=[
            pltpu.VMEM((2,) + info.shape, jnp.int32),
            pltpu.VMEM((2, 2, seq, width), bf),
            pltpu.VMEM((2, 2, seq, 128), bf),
            pltpu.VMEM(block[2:] + (width,), bf),
            pltpu.VMEM(block[2:] + (width,), bf),
            pltpu.VMEM(block[2:] + (128,), bf),
            DMA((4,)),
            DMA((4,)),
            DMA((3, n_expert)),
            DMA((3, n_expert)),
            DMA((3, ny, n_expert)),
            DMA((3, ny, n_expert)),
            DMA((3, ny)),
            DMA((3, ny)),
        ],
        name="spread",
        compiler_params=pltpu.CompilerParams(
            collective_id=1, has_side_effects=True, vmem_limit_bytes=48 << 20
        ),
    )(info, cot, moe, weights)


def gather_back_kernel(sizes, p0_ref, p1_ref, q_out, r1, stage, r2, final, s1, t1, s2, t2, s3, t3, s4, t4):
    me = Place(*sizes)
    greet(column_peers(me))
    c, mate = me.c, me.at(c=1 - me.c)
    p_refs = (p0_ref, p1_ref)
    count = 2
    ys = [(me.y + k) % me.ny for k in range(me.ny)]
    order = list(range(1, me.n_expert)) + [0]
    first = {}
    for i in range(count):
        for k in list(range(1, me.ny)) + [0]:
            y = ys[k]
            first[i, k] = remote(
                p_refs[i].at[1 - c, y], r1.at[i, y], s1.at[i, k], t1.at[i, k], mate
            )
    second, third, fourth = {}, {}, []
    for i in range(count):
        for k in range(1, me.ny):
            first[i, k].wait_recv()
            for j in order:
                e = (me.e + j) % me.n_expert
                total = p_refs[i][c, ys[k], e].astype(jnp.float32) + r1[i, ys[k], e].astype(jnp.float32)
                stage[i, k - 1, e] = total.astype(jnp.bfloat16)
                second[i, k, j] = remote(
                    stage.at[i, k - 1, e], r2.at[i, k - 1, e], s2.at[i, k - 1, j], t2.at[i, k - 1, j],
                    me.at(y=ys[k]),
                )
    for i in range(count):
        first[i, 0].wait_recv()
        for j in order:
            e = (me.e + j) % me.n_expert
            total = p_refs[i][c, me.y, e].astype(jnp.float32) + r1[i, me.y, e].astype(jnp.float32)
            for k in range(1, me.ny):
                second[i, k, j].wait_recv()
                total = total + r2[i, k - 1, e].astype(jnp.float32)
            if j:
                final[i, e] = total.astype(jnp.bfloat16)
                third[i, j] = remote(
                    final.at[i, e], q_out.at[i, c, me.e], s3.at[i, j], t3.at[i, j], me.at(e=e)
                )
            else:
                q_out[i, c, me.e] = total.astype(jnp.bfloat16)
    for i in range(count):
        for j in order[:-1]:
            third[i, j].wait_recv()
        block = q_out.at[i, c]
        fourth.append(remote(block, block, s4.at[i], t4.at[i], mate))
    for copy in fourth:
        copy.wait()
    for copies in (first, second, third):
        for copy in copies.values():
            copy.wait_send()


def gather_back(sizes, first, second):
    n_expert, n_dp = sizes
    count = 2
    _, ny, _, rows, width = first.shape
    bf = jnp.bfloat16
    most = max(ny - 1, 1)
    return pl.pallas_call(
        functools.partial(gather_back_kernel, sizes),
        out_shape=jax.ShapeDtypeStruct((count, 2, n_expert, rows, width), bf),
        in_specs=[VMEM] * 2,
        out_specs=VMEM,
        scratch_shapes=[
            pltpu.VMEM((count, ny, n_expert, rows, width), bf),
            pltpu.VMEM((count, most, n_expert, rows, width), bf),
            pltpu.VMEM((count, most, n_expert, rows, width), bf),
            pltpu.VMEM((count, n_expert, rows, width), bf),
            DMA((count, ny)),
            DMA((count, ny)),
            DMA((count, most, n_expert)),
            DMA((count, most, n_expert)),
            DMA((count, n_expert)),
            DMA((count, n_expert)),
            DMA((count,)),
            DMA((count,)),
        ],
        name="gather_back",
        compiler_params=pltpu.CompilerParams(
            collective_id=2, has_side_effects=True, vmem_limit_bytes=48 << 20
        ),
    )(first, second)


def reduce_kernel(
    sizes, pieces, left_ref, right_ref, small_ref, out, small_out,
    buf_a, buf_b, acc, part0, part1, part2, got0, got1, got2, half, small_half, small_got,
    fs, fr, os, ps, pr, gs, gr, ms, mr, cs, cr, ss, sr,
):
    me = Place(*sizes)
    c, mate = me.c, me.at(c=1 - me.c)
    n = me.nx
    seq = right_ref.shape[1]
    total_rows = out.shape[1]
    is0 = c == 0
    pair = jnp.where(is0, me.x, me.y)
    other = jnp.where(is0, me.y, me.x)
    lo, hi, nh = pair % 2, pair // 2, n // 2

    def along(pair_at, other_at, z=None):
        return me.at(x=jnp.where(is0, pair_at, other_at), y=jnp.where(is0, other_at, pair_at), z=z)

    flip_x, flip_y = me.x + 1 - 2 * (me.x % 2), me.y + 1 - 2 * (me.y % 2)
    dims = [
        (n, other, lambda q: along(pair, q)),
        (nh, hi, lambda q: along(q * 2 + lo, other)),
        (me.nz, me.z, lambda q: me.at(z=q)),
    ]
    parts, gots = [part0, part1, part2], [got0, got1, got2]
    levels = [i for i, d in enumerate(dims) if d[0] > 1]
    x_peers = [me.at(x=(me.x + k) % n) for k in range(1, n)]
    y_peers = [me.at(y=(me.y + k) % n) for k in range(1, n)]
    z_peers = [me.at(z=(me.z + k) % me.nz) for k in range(1, me.nz)]
    greet(
        [mate, me.at(x=flip_x, c=1 - c), me.at(y=flip_y, c=1 - c)] + x_peers + y_peers + z_peers
    )

    def slot_a(slot):
        return buf_a.at[:, pl.ds(pl.multiple_of(slot * seq, seq), seq)]

    def slot_b(slot):
        return buf_b.at[pl.ds(pl.multiple_of(slot * seq, seq), seq), :]

    targets = [
        (mate, 1 - c, other % 2, c),
        (me.at(x=flip_x, c=0), 0, flip_x % 2, 2 + c),
        (me.at(y=flip_y, c=1), 1, flip_y % 2, 2 + c),
    ]
    factor = []
    for i, (device, role, parity, slot) in enumerate(targets):
        a, b = jnp.where(role == 0, 0, parity), role * 2 + parity
        factor.append(remote(left_ref.at[a], slot_a(slot), fs.at[i, 0], fr.at[slot, 0], device))
        factor.append(remote(right_ref.at[b], slot_b(slot), fs.at[i, 1], fr.at[slot, 1], device))
    own = [
        pltpu.make_async_copy(left_ref.at[jnp.where(is0, 0, lo)], slot_a(c), os.at[0]),
        pltpu.make_async_copy(right_ref.at[c * 2 + lo], slot_b(c), os.at[1]),
    ]
    for copy in own:
        copy.start()
    rows_s = half.shape[0]
    small = [remote(small_ref.at[pl.ds((1 - c) * rows_s, rows_s)], half, ss.at[0], sr.at[0], mate)]
    small[0].wait_recv()
    small_half[0] = small_ref[pl.ds(c * rows_s, rows_s)] + half[...]
    slot = 1
    for level, (count, index, peer) in enumerate(
        ((n, me.x, lambda q: me.at(x=q)), (n, me.y, lambda q: me.at(y=q)), (me.nz, me.z, lambda q: me.at(z=q)))
    ):
        if count > 1:
            copies = []
            for k in range(1, count):
                copies.append(
                    remote(
                        small_half.at[level], small_got.at[level, index], ss.at[slot], sr.at[slot],
                        peer((index + k) % count),
                    )
                )
                slot += 1
            small_got[level, index] = small_half[level]
            for copy in copies:
                copy.wait_recv()
            small += copies
            total = small_got[level, 0]
            for k in range(1, count):
                total = total + small_got[level, k]
        else:
            total = small_half[level]
        if level < 2:
            small_half[level + 1] = total
        else:
            small_out[pl.ds(c * rows_s, rows_s)] = total
    block = small_out.at[pl.ds(c * rows_s, rows_s)]
    small.append(remote(block, block, ss.at[slot], sr.at[slot], mate))
    for where in (1 - c, 2, 3):
        for i, (src, dst) in enumerate(((left_ref, slot_a(where)), (right_ref, slot_b(where)))):
            pltpu.make_async_remote_copy(
                src_ref=src.at[0], dst_ref=dst, send_sem=fs.at[0, i], recv_sem=fr.at[where, i],
                device_id=mate, device_id_type=MESH,
            ).wait_recv()
    for copy in own:
        copy.wait()

    rows_k = total_rows // pieces
    matrix = c * 2 + lo
    pending = {}

    def multiply(k):
        acc[k] = jnp.dot(
            buf_a[k * rows_k : (k + 1) * rows_k, :], buf_b[...], preferred_element_type=jnp.float32
        )
        push(k, 0, rows_k)

    def push(k, at, rows):
        level = levels[at]
        count, index, peer = dims[level]
        size = rows // count
        copies = []
        for s in range(1, count):
            to = (index + s) % count
            parts[level][k, s - 1] = acc[k, pl.ds(pl.multiple_of(to * size, 8), size), :].astype(jnp.bfloat16)
            copies.append(
                remote(
                    parts[level].at[k, s - 1], gots[level].at[k, s - 1],
                    ps.at[level, k, s - 1], pr.at[level, k, s - 1], peer(to),
                )
            )
        pending["push", at, k] = copies

    def rows_at(at):
        rows = rows_k
        for i in range(at):
            rows //= dims[levels[i]][0]
        return rows

    def add(k, at):
        level = levels[at]
        count, index, _ = dims[level]
        size = rows_at(at) // count
        for copy in pending["push", at, k]:
            copy.wait_recv()
        total = acc[k, pl.ds(pl.multiple_of(index * size, 8), size), :]
        for s in range(1, count):
            total = total + gots[level][k, s - 1].astype(jnp.float32)
        if at + 1 < len(levels):
            acc[k, :size, :] = total
            push(k, at + 1, size)
        else:
            out[matrix, pl.ds(offset(k, at), size), :] = total.astype(jnp.bfloat16)
            share(k, at)

    def offset(k, at):
        start, rows = k * rows_k, rows_k
        for i in range(at + 1):
            count, index, _ = dims[levels[i]]
            rows //= count
            start = start + index * rows
        return pl.multiple_of(start, 8)

    def share(k, at):
        level = levels[at]
        count, index, peer = dims[level]
        size = rows_at(at) // count
        block = out.at[matrix, pl.ds(offset(k, at), size), :]
        pending["share", at, k] = [
            remote(block, block, gs.at[level, k, s - 1], gr.at[level, k, s - 1], peer((index + s) % count))
            for s in range(1, count)
        ]

    def shared(k, at):
        for copy in pending["share", at, k]:
            copy.wait_recv()
        if at:
            share(k, at - 1)
        else:
            block = out.at[matrix, pl.ds(k * rows_k, rows_k), :]
            pending["mate", k] = remote(
                block, block, ms.at[k], mr.at[k], along(pair + 1 - 2 * lo, other)
            )

    def across(k):
        pending["mate", k].wait_recv()
        block = out.at[pl.ds(2 * c, 2), pl.ds(k * rows_k, rows_k), :]
        pending["core", k] = remote(block, block, cs.at[k], cr.at[k], mate)

    steps = [multiply]
    steps += [functools.partial(add, at=i) for i in range(len(levels))]
    steps += [functools.partial(shared, at=i) for i in reversed(range(len(levels)))]
    steps += [across, lambda k: pending["core", k].wait_recv()]
    for t in range(pieces + len(steps) - 1):
        for p in reversed(range(len(steps))):
            if 0 <= t - p < pieces:
                steps[p](t - p)
    small[-1].wait_recv()
    for copy in factor + small:
        copy.wait_send()
    for copies in pending.values():
        for copy in copies if isinstance(copies, list) else [copies]:
            copy.wait_send()


def reduce_all(sizes, left, right, small):
    n_expert, n_dp = sizes
    nz = math.gcd(n_expert, 4)
    n = n_expert // nz
    nh = n // 2
    assert n == n_dp // 2
    width, seq = left.shape[1:]
    pieces = 4
    rows_k = width // pieces
    bf, f32 = jnp.bfloat16, jnp.float32
    rows_s = small.shape[0] // 2
    sizes_at = [rows_k // n, rows_k // (n * nh), rows_k // (n * nh * nz)]
    counts = [max(n - 1, 1), max(nh - 1, 1), max(nz - 1, 1)]
    most = max(counts)
    boxes = [pltpu.VMEM((pieces, q, s, width), bf) for q, s in zip(counts, sizes_at)]
    smalls = 2 * n + nz
    return pl.pallas_call(
        functools.partial(reduce_kernel, sizes, pieces),
        out_shape=(
            jax.ShapeDtypeStruct((4, width, width), bf),
            jax.ShapeDtypeStruct(small.shape, f32),
        ),
        in_specs=[VMEM] * 3,
        out_specs=(VMEM, VMEM),
        scratch_shapes=[
            pltpu.VMEM((width, 4 * seq), bf),
            pltpu.VMEM((4 * seq, width), bf),
            pltpu.VMEM((pieces, rows_k, width), f32),
            *boxes,
            *boxes,
            pltpu.VMEM((rows_s, width), f32),
            pltpu.VMEM((3, rows_s, width), f32),
            pltpu.VMEM((3, max(n, nz), rows_s, width), f32),
            DMA((3, 2)),
            DMA((4, 2)),
            DMA((2,)),
            DMA((3, pieces, most)),
            DMA((3, pieces, most)),
            DMA((3, pieces, most)),
            DMA((3, pieces, most)),
            DMA((pieces,)),
            DMA((pieces,)),
            DMA((pieces,)),
            DMA((pieces,)),
            DMA((smalls,)),
            DMA((smalls,)),
        ],
        name="reduce_all",
        compiler_params=pltpu.CompilerParams(
            collective_id=3, has_side_effects=True, vmem_limit_bytes=56 << 20
        ),
    )(left, right, small)


def rms_scale(values):
    return lax.rsqrt(jnp.mean(values * values, axis=-1, keepdims=True) + epsilon)


def bucket_hot(seq_len, buckets):
    position = jnp.arange(seq_len, dtype=jnp.int32)
    relative = position[None, :] - position[:, None]
    distance = jnp.abs(relative)
    far_bucket = jnp.full_like(distance, 8)
    for threshold in bucket_edges:
        far_bucket = far_bucket + (distance >= threshold).astype(jnp.int32)
    bucketed = jnp.where(distance < 8, distance, far_bucket) + 16 * (relative > 0).astype(jnp.int32)
    bucket_ids = jnp.arange(buckets, dtype=jnp.int32)
    return (bucketed[None, :, :] == bucket_ids[:, None, None]).astype(jnp.float32)


def gated_product(gate_pre, up_pre):
    return jax.nn.gelu(gate_pre, approximate=True) * up_pre


def dot32(pattern, left, right):
    return jnp.einsum(pattern, left, right, preferred_element_type=jnp.float32)


def shards(
    layer_in, routes, queue_slots, norm_attn, w_query, w_key, w_value, w_out, rel_table,
    norm_moe, router, w_gate, w_up, w_down, cotangent,
):
    bf, f32 = jnp.bfloat16, jnp.float32
    seq_len, width = layer_in.shape
    buckets, heads = rel_table.shape
    expert_count = router.shape[1]
    sizes = (lax.axis_size("expert"), lax.axis_size("dp"))
    n_expert, n_dp = sizes
    assert w_gate.shape[0] == 2 and expert_count == 2 * n_expert
    group_len = seq_len // MICRO
    capacity = (5 * group_len + 2 * expert_count - 1) // (2 * expert_count)
    split_heads = (seq_len, heads, width // heads)
    layer_rows = layer_in.astype(f32)
    inv_attn = rms_scale(layer_rows)
    normed_attn = layer_rows * inv_attn
    attn_in = (normed_attn * norm_attn).astype(bf)
    query_heads = dot32("sd,de->se", attn_in, w_query).astype(bf).reshape(split_heads)
    key_heads = dot32("sd,de->se", attn_in, w_key).astype(bf).reshape(split_heads)
    value_heads = dot32("sd,de->se", attn_in, w_value).astype(bf).reshape(split_heads)
    one_hot = bucket_hot(seq_len, buckets)
    bias = jnp.einsum("bij,bh->hij", one_hot, rel_table, precision=highest)
    scores = dot32("ihd,jhd->hij", query_heads, key_heads) + bias
    exponent = jnp.exp(scores - jnp.max(scores, axis=-1, keepdims=True))
    probs = exponent / jnp.sum(exponent, axis=-1, keepdims=True)
    probs_low = probs.astype(bf)
    context = dot32("hij,jhd->ihd", probs_low, value_heads).astype(bf).reshape(seq_len, width)
    residual = layer_rows + dot32("se,ed->sd", context, w_out)
    inv_moe = rms_scale(residual)
    normed_moe = residual * inv_moe
    moe_in = normed_moe * norm_moe
    logits = jnp.dot(moe_in, router, precision=highest)
    gate_prob = jax.nn.softmax(logits, axis=-1)
    expert_ids = jnp.arange(expert_count, dtype=jnp.int32)
    first_hot = (routes[:, 0:1] == expert_ids).astype(f32)
    second_hot = (routes[:, 1:2] == expert_ids).astype(f32)
    prob_first = jnp.sum(gate_prob * first_hot, axis=-1, keepdims=True)
    prob_second = jnp.sum(gate_prob * second_hot, axis=-1, keepdims=True)
    weight_first = prob_first / (prob_first + prob_second)
    weight_second = prob_second / (prob_first + prob_second)
    weights = jnp.concatenate([weight_first, weight_second], axis=1)

    info = jnp.concatenate([routes.T, queue_slots.T, jnp.zeros((4, seq_len), jnp.int32)])
    grad_in, rows_in, weight_in = spread(
        sizes, MICRO, capacity, info, cotangent, moe_in.astype(bf), weights
    )
    block = grad_in.shape[:-1]
    expert_rows = rows_in.reshape(2, -1, width)
    slot_weight = jnp.sum(weight_in[..., :3].astype(f32), axis=-1).reshape(2, -1, 1)
    grad_rows = (slot_weight * grad_in.reshape(2, -1, width).astype(f32)).astype(bf)
    gate_pre = dot32("jrd,jdf->jrf", expert_rows, w_gate)
    up_pre = dot32("jrd,jdf->jrf", expert_rows, w_up)
    product, pullback = jax.vjp(gated_product, gate_pre, up_pre)
    hidden = product.astype(bf)
    partial_out = dot32("jrf,jfd->jrd", hidden, w_down).astype(bf)
    hidden_grad = dot32("jrd,jfd->jrf", grad_rows, w_down)
    gate_grad, up_grad = [g.astype(bf) for g in pullback(hidden_grad)]
    rows_grad = dot32("jrf,jdf->jrd", gate_grad, w_gate) + dot32("jrf,jdf->jrd", up_grad, w_up)
    grad_w_gate = dot32("jrd,jrf->jdf", expert_rows, gate_grad)
    grad_w_up = dot32("jrd,jrf->jdf", expert_rows, up_grad)
    grad_w_down = dot32("jrf,jrd->jfd", hidden, grad_rows)
    back = gather_back(
        sizes, partial_out.reshape(block + (width,)), rows_grad.astype(bf).reshape(block + (width,))
    )
    back = back.reshape(2, -1, width)

    core = lax.axis_index("dp") % 2
    per_core = MICRO * capacity
    token = jnp.arange(seq_len, dtype=jnp.int32)[:, None]
    place = (routes % 2) * (n_expert * 2 * per_core) + (routes // 2) * (2 * per_core)
    place = place + core * per_core + (token // group_len) * capacity + queue_slots
    place = jnp.where(queue_slots >= 0, place, -1)
    slot_ids = jnp.arange(2 * n_expert * 2 * per_core, dtype=jnp.int32)
    select_first = (place[:, 0:1] == slot_ids).astype(bf)
    select_second = (place[:, 1:2] == slot_ids).astype(bf)
    picked_first = dot32("tp,pd->td", select_first, back[0])
    picked_second = dot32("tp,pd->td", select_second, back[0])
    moe = weight_first * picked_first + weight_second * picked_second
    layer_out = (residual + moe).astype(bf)
    cot_rows = cotangent.astype(f32)
    grad_weight_first = jnp.sum(cot_rows * picked_first, axis=-1, keepdims=True)
    grad_weight_second = jnp.sum(cot_rows * picked_second, axis=-1, keepdims=True)
    grad_from_slots = dot32("tp,pd->td", select_first + select_second, back[1])
    mean_grad = weight_first * grad_weight_first + weight_second * grad_weight_second
    logit_first = weight_first * (grad_weight_first - mean_grad)
    logit_second = weight_second * (grad_weight_second - mean_grad)
    grad_logits = logit_first * first_hot + logit_second * second_hot
    grad_router = jnp.einsum("sd,se->ed", moe_in, grad_logits, precision=highest)
    grad_moe_in = grad_from_slots + jnp.einsum("se,de->sd", grad_logits, router, precision=highest)
    grad_norm_moe = jnp.sum(grad_moe_in * normed_moe, axis=0)
    grad_normed = grad_moe_in * norm_moe
    grad_residual = cot_rows + inv_moe * (
        grad_normed - normed_moe * jnp.mean(grad_normed * normed_moe, axis=-1, keepdims=True)
    )
    grad_attn_low = grad_residual.astype(bf)
    grad_context = dot32("sd,ed->se", grad_attn_low, w_out).astype(bf).reshape(split_heads)
    grad_values = dot32("hij,ihd->jhd", probs_low, grad_context).astype(bf).reshape(seq_len, width)
    grad_probs = dot32("ihd,jhd->hij", grad_context, value_heads)
    grad_scores = probs * (grad_probs - jnp.sum(probs * grad_probs, axis=-1, keepdims=True))
    grad_rel_table = jnp.einsum("bij,hij->bh", one_hot, grad_scores, precision=highest)
    scores_low = grad_scores.astype(bf)
    grad_queries = dot32("hij,jhd->ihd", scores_low, key_heads).astype(bf).reshape(seq_len, width)
    grad_keys = dot32("hij,ihd->jhd", scores_low, query_heads).astype(bf).reshape(seq_len, width)
    grad_attn_in = dot32("se,de->sd", grad_queries, w_query)
    grad_attn_in = grad_attn_in + dot32("se,de->sd", grad_keys, w_key)
    grad_attn_in = grad_attn_in + dot32("se,de->sd", grad_values, w_value)
    grad_norm_attn = jnp.sum(grad_attn_in * normed_attn, axis=0)
    grad_normed_attn = grad_attn_in * norm_attn
    grad_input = grad_residual + inv_attn * (
        grad_normed_attn
        - normed_attn * jnp.mean(grad_normed_attn * normed_attn, axis=-1, keepdims=True)
    )
    table = grad_rel_table.reshape(-1)
    small = jnp.concatenate(
        [
            grad_router,
            grad_norm_attn[None],
            grad_norm_moe[None],
            jnp.pad(table, (0, width - table.size))[None],
        ]
    )
    small = jnp.pad(small, ((0, -small.shape[0] % 16), (0, 0)))
    sums, small = reduce_all(
        sizes,
        jnp.stack([attn_in.T, context.T]),
        jnp.stack([grad_queries, grad_keys, grad_values, grad_attn_low]),
        small,
    )
    matrices = [sums[i].astype(f32) for i in range(4)]
    return (
        layer_out, grad_input, small[expert_count], *matrices,
        small[expert_count + 2, : table.size].reshape(buckets, heads),
        small[expert_count + 1], small[:expert_count].T, grad_w_gate, grad_w_up, grad_w_down,
    )


def solution(mesh):
    in_specs = (
        P(("expert", "dp"), None),
        P(("expert", "dp"), None),
        P(("expert", "dp"), None),
        P(),
        P(),
        P(),
        P(),
        P(),
        P(),
        P(),
        P(),
        P("expert", None, "dp"),
        P("expert", None, "dp"),
        P("expert", "dp", None),
        P(("expert", "dp"), None),
    )
    out_specs = (
        P(("expert", "dp"), None),
        P(("expert", "dp"), None),
        P(),
        P(),
        P(),
        P(),
        P(),
        P(),
        P(),
        P(),
        P("expert", None, "dp"),
        P("expert", None, "dp"),
        P("expert", "dp", None),
    )
    return jax.shard_map(shards, mesh=mesh, in_specs=in_specs, out_specs=out_specs, check_vma=False)
```

time: 690 us -> 331 us (0.48)
  waiting for transfers between devices: 332 us -> 0 us
  Pallas kernels: 0 us -> 202 us
  blocking collectives: 173 us -> 0 us
  local copies, waits for them, and re-layouts: 56.4 us -> 20.4 us
  other arithmetic: 18 us -> 34 us
  between operations: 15.7 us -> 1.79 us
  matrix products: 80.9 us -> 67.4 us
  starting transfers between devices: 7.89 us -> 0 us
    psum x1 -> x0, waiting for transfers between devices: 217 us -> none  [shards(): lax.psum((grad_norm_attn, grad_w_query, grad_w_key, grad_w_value, grad_w_...]
    pallas_call x0 -> x3, Pallas kernels: none -> 202 us  [the longest x1 106 us: reduce_all(): pl.pallas_call(functools.partial(reduce_kernel, sizes, pieces), out_shape...]
    all_to_all x2 -> x0, blocking collectives: 132 us -> none  [the longest x1 67 us: shards(): lax.all_to_all(spread, ('expert', 'dp'), split_axis=2, concat_axis=0, til...]
    all_to_all x2 -> x0, waiting for transfers between devices: 115 us -> none  [the longest x1 58.3 us: shards(): lax.all_to_all(rows_grad.astype(jnp.bfloat16), ('expert', 'dp'), split_ax...]
    psum x1 -> x0, blocking collectives: 40.5 us -> none  [shards(): lax.psum((grad_norm_attn, grad_w_query, grad_w_key, grad_w_value, grad_w_...]
    unnamed x189 -> x123, local copies, waits for them, and re-layouts: 20.6 us -> 6.7 us
    convert_element_type x2 -> x3, other arithmetic: 1.31 us -> 13.7 us  [the longest x1 10.2 us: shards(): matrices = [sums[i].astype(f32) for i in range(4)]]
    dot_general x36 -> x29, matrix products: 77.9 us -> 66.2 us  [the longest x26 62.1 us: dot32(): return jnp.einsum(pattern, left, right, preferred_element_type=jnp.float32)]
  transfers between devices with their start and end apart: 3 -> 0, of which waited for: 3 -> 0; matrix products, arithmetic and copies ran while one was open for 5% -> 0% of each run, Pallas kernels for 0% -> 0%
where the time goes in v1:
time: 331 us; the launch traced here: 325 us
  Pallas kernels  202 us (61%)
  matrix products  67.4 us (20%)
  other arithmetic  34 us (10%)
  local copies, waits for them, and re-layouts  20.4 us (6%)
    pallas_call x1, Pallas kernels, reduce_all(): pl.pallas_call(functools.partial(reduce_kernel, sizes, pieces), out_shape...  106 us
    dot_general x26, matrix products, dot32(): return jnp.einsum(pattern, left, right, preferred_element_type=jnp.float32)  62.1 us
    pallas_call x1, Pallas kernels, spread(): pl.pallas_call(functools.partial(spread_kernel, sizes, (micro, cap, per_c...  48.6 us
    pallas_call x1, Pallas kernels, gather_back(): pl.pallas_call(functools.partial(gather_back_kernel, sizes), out_shape=ja...  47.2 us
    mul x1, other arithmetic, shards(): probs * (grad_probs - jnp.sum(probs * grad_probs, axis=-1, keepdims=True))  10.7 us
    convert_element_type x1, other arithmetic, shards(): matrices = [sums[i].astype(f32) for i in range(4)]  10.2 us
    unnamed x123, local copies, waits for them, and re-layouts  6.7 us

profile of v1, /device:TPU:1, one launch (start us, length us, event | category | flops | bytes accessed | tf_op | source)
XLA Modules:
  0.0 325.3 jit_solution(13458867512651780972)
XLA Ops:
  0.7 1.2 fusion.26
  1.9 2.9 convolution_convert_fusion.7
  6.0 2.9 convolution_convert_fusion.6
  8.9 1.8 copy.75
  10.8 1.7 fusion.10
  12.5 2.5 copy.76
  15.0 1.8 convolution_add_fusion
  17.8 1.2 fusion.90
  20.3 2.8 convolution_convert_fusion.5
  23.2 2.3 multiply_reduce_fusion.3
  30.1 48.6 %spread.1 = (bf16[2,2,8,40,1024]{4,3,2,1,0:T(8,128)(2,1)S(1)}, bf16[2,2,8,40,1024]{4,3,2,1,0:T(8,128)(2,1)S(1)}, bf16[2,2,8,40,128]{4,3,2,1,0:T(8,128)(2,1)S(1)}) custom-call(s32[8,128]{1,0:T(8,128)S(1)} %add_add_fusion.info_ref, bf16[128,1024]{1,0:T(8,128)(2,1)S(1)} %copy-done.3, bf16[128,1024]{1,0:T(8,128)(2,1)S(1)} %multiply_convert_fusion.2.moe_ref, ...), custom_call_target="tpu_custom_call" | custom-call | tf_op jit(solution)/shard_map/spread/pallas_call | solution.py:178
  78.7 1.5 copy-done.2
  80.2 1.5 copy-done.4
  82.0 2.4 fusion.1
  84.6 5.1 %fusion.92 = f32[2,640,704]{1,2,0:T(8,128)S(1)} fusion(bf16[2,640,1024]{2,1,0:T(8,128)(2,1)S(1)} %bitcast.131, bf16[2,1024,704]{1,2,0:T(8,128)(2,1)} %param.26), kind=kOutput, calls=%fused_computation.173 | convolution fusion | flops 1845493760 | bytes 9109504 | tf_op jit(solution)/shard_map/jrd,jdf->jrf/dot_general | solution.py:566
  89.7 2.4 fusion.93
  92.2 5.1 %multiply_convert_fusion = (bf16[2,640,704]{1,2,0:T(8,128)(2,1)S(1)}, bf16[2,640,704]{1,2,0:T(8,128)(2,1)S(1)}, bf16[2,640,704]{1,2,0:T(8,128)(2,1)S(1)}) fusion(f32[2,640,704]{1,2,0:T(8,128)S(1)} %fusion.92, f32[2,640,704]{1,2,0:T(8,128)S(1)} %fusion.93, bf16[2,640,1024]{2,1,0:T(8,128)(2,1)S(1)} %fusion.1, bf16[2,704,1024]{2,1,0:T(8,128)(2,1)S(1)} %copy-done), kind=kOutput, calls=%fused_computation.13 | convolution fusion | flops 1868922880 | bytes 18120704 | tf_op jit(solution)/shard_map/jrd,jfd->jrf/dot_general | solution.py:566
  97.3 2.3 fusion.94
  99.6 3.8 %add_convert_fusion = bf16[2,640,1024]{2,1,0:T(8,128)(2,1)} fusion(f32[2,640,1024]{2,1,0:T(8,128)S(1)} %fusion.94, bf16[2,640,704]{1,2,0:T(8,128)(2,1)S(1)} %get-tuple-element.79, bf16[2,1024,704]{1,2,0:T(8,128)(2,1)S(1)} %copy-done.55), kind=kOutput, calls=%fused_computation.3 | convolution fusion | flops 1848115200 | bytes 12550144 | tf_op jit(solution)/shard_map/jrf,jdf->jrd/dot_general | solution.py:566
  103.4 2.3 convolution_convert_fusion
  105.6 47.2 %gather_back.1 = bf16[2,2,8,40,1024]{4,3,2,1,0:T(8,128)(2,1)S(1)} custom-call(bf16[2,2,8,40,1024]{4,3,2,1,0:T(8,128)(2,1)S(1)} %bitcast.130, bf16[2,2,8,40,1024]{4,3,2,1,0:T(8,128)(2,1)} %bitcast.138), custom_call_target="tpu_custom_call" | custom-call | tf_op jit(solution)/shard_map/gather_back/pallas_call | solution.py:270
  152.9 1.8 fusion.88
  154.8 1.9 fusion.36
  163.0 2.9 convolution_convert_fusion.1
  166.3 10.7 %subtract_multiply_fusion = f32[16,128,128]{1,2,0:T(8,128)S(1)} fusion(f32[16,128,128]{1,2,0:T(8,128)S(1)} %get-tuple-element.103, f32[16,128]{1,0:T(8,128)S(1)} %get-tuple-element.102, f32[16,128,128]{1,2,0:T(8,128)S(1)} %copy-done.19, f32[16,128]{1,0:T(8,128)S(1)} %get-tuple-element.94), kind=kLoop, calls=%fused_computation.41 | loop fusion | flops 786432 | bytes 3162112 | tf_op jit(solution)/shard_map/mul | solution.py:668
  180.8 1.5 fusion.25
  182.9 1.2 fusion.13
  188.6 105.9 %reduce_all.1 = (bf16[4,1024,1024]{2,1,0:T(8,128)(2,1)}, f32[32,1024]{1,0:T(8,128)}) custom-call(bf16[2,1024,128]{2,1,0:T(8,128)(2,1)} %copy.89.left_ref, bf16[4,128,1024]{2,1,0:T(8,128)(2,1)} %pad_maximum_fusion.right_ref, f32[32,1024]{1,0:T(8,128)} %select_maximum_fusion.small_ref), custom_call_target="tpu_custom_call" | custom-call | tf_op jit(solution)/shard_map/reduce_all/pallas_call | solution.py:507
  294.6 10.2 %bitcast_convert_fusion = (f32[1024,1024]{1,0:T(8,128)}, f32[1024,1024]{1,0:T(8,128)}, f32[1024,1024]{1,0:T(8,128)}, f32[1024,1024]{1,0:T(8,128)}) fusion(bf16[4,1024,1024]{2,1,0:T(8,128)(2,1)} %get-tuple-element.22), kind=kLoop, calls=%fused_computation.16 | loop fusion | flops 4194304 | bytes 25165824 | tf_op jit(solution)/shard_map/convert_element_type | solution.py:698
  306.8 7.4 %fusion.96 = f32[2,704,1024]{2,1,0:T(8,128)} fusion(bf16[2,640,704]{1,2,0:T(8,128)(2,1)} %copy-done.60, bf16[2,640,1024]{2,1,0:T(8,128)(2,1)} %copy-done.21), kind=kOutput, calls=%fused_computation.177 | convolution fusion | flops 1845493760 | bytes 10190848 | tf_op jit(solution)/shard_map/jrf,jrd->jfd/dot_general | solution.py:566
  315.2 4.9 %fusion.97 = f32[2,1024,704]{1,2,0:T(8,128)} fusion(bf16[2,640,704]{1,2,0:T(8,128)(2,1)S(1)} %copy-done.59, bf16[2,640,1024]{2,1,0:T(8,128)(2,1)S(1)} %bitcast.133), kind=kOutput, calls=%fused_computation.178 | convolution fusion | flops 1845493760 | bytes 10190848 | tf_op jit(solution)/shard_map/jrd,jrf->jdf/dot_general | solution.py:566
  320.1 4.9 %fusion.98 = f32[2,1024,704]{1,2,0:T(8,128)} fusion(bf16[2,640,704]{1,2,0:T(8,128)(2,1)S(1)} %copy-done.57, bf16[2,640,1024]{2,1,0:T(8,128)(2,1)S(1)} %bitcast.134), kind=kOutput, calls=%fused_computation.179 | convolution fusion | flops 1845493760 | bytes 10190848 | tf_op jit(solution)/shard_map/jrd,jrf->jdf/dot_general | solution.py:566
  (176 shorter events, 26.9 us)
Async XLA Ops:
  0.6 91.5 %copy-start = (bf16[2,704,1024]{2,1,0:T(8,128)(2,1)S(1)}, bf16[2,704,1024]{2,1,0:T(8,128)(2,1)}, u32[]{:S(2)}) copy-start(bf16[2,704,1024]{2,1,0:T(8,128)(2,1)} %param.28) | copy-start | bytes 8650756
  0.7 5.3 %copy-start.9 = (bf16[128,1024]{1,0:T(8,128)(2,1)S(1)}, bf16[128,1024]{1,0:T(8,128)(2,1)}, u32[]{:S(2)}) copy-start(bf16[128,1024]{1,0:T(8,128)(2,1)} %param.15) | copy-start | bytes 786436
  0.7 5.3 %copy-start.34 = (f32[1024]{0:T(1024)S(1)}, f32[1024]{0:T(1024)}, u32[]{:S(2)}) copy-start(f32[1024]{0:T(1024)} %param.18) | copy-start | bytes 12292
  1.9 17.1 %copy-start.39 = (f32[128]{0:T(128)}, f32[128]{0:T(128)S(1)}, u32[]{:S(2)}) copy-start(f32[128]{0:T(128)S(1)} %add_rsqrt_fusion.1) | copy-start | bytes 1540
  1.9 8.8 %copy-start.43 = (f32[32,16]{0,1:T(8,128)S(1)}, f32[32,16]{0,1:T(8,128)}, u32[]{:S(2)}) copy-start(f32[32,16]{0,1:T(8,128)} %param.23) | copy-start | bytes 6148
  6.0 9.1 %copy-start.22 = (bf16[128,1024]{0,1:T(8,128)(2,1)}, bf16[128,1024]{0,1:T(8,128)(2,1)S(1)}, u32[]{:S(2)}) copy-start(bf16[128,1024]{0,1:T(8,128)(2,1)S(1)} %copy.74) | copy-start | bytes 786436
  15.0 4.0 %copy-start.14 = (bf16[1024,1024]{1,0:T(8,128)(2,1)S(1)}, bf16[1024,1024]{1,0:T(8,128)(2,1)}, u32[]{:S(2)}) copy-start(bf16[1024,1024]{1,0:T(8,128)(2,1)} %param.21) | copy-start | bytes 6291460
  23.2 3.0 copy-start.41
  23.2 6.9 %copy-start.3 = (bf16[128,1024]{1,0:T(8,128)(2,1)S(1)}, bf16[128,1024]{1,0:T(8,128)(2,1)}, u32[]{:S(2)}) copy-start(bf16[128,1024]{1,0:T(8,128)(2,1)} %cot_ref.1) | copy-start | bytes 786436
  84.4 7.7 %copy-start.21 = (bf16[2,640,1024]{2,1,0:T(8,128)(2,1)}, bf16[2,640,1024]{2,1,0:T(8,128)(2,1)S(1)}, u32[]{:S(2)}) copy-start(bf16[2,640,1024]{2,1,0:T(8,128)(2,1)S(1)} %fusion.1) | copy-start | bytes 7864324
  84.6 5.1 %copy-start.55 = (bf16[2,1024,704]{1,2,0:T(8,128)(2,1)S(1)}, bf16[2,1024,704]{1,2,0:T(8,128)(2,1)}, u32[]{:S(2)}) copy-start(bf16[2,1024,704]{1,2,0:T(8,128)(2,1)} %param.27) | copy-start | bytes 8650756
  92.1 5.2 %copy-start.54 = (bf16[2,1024,704]{1,2,0:T(8,128)(2,1)S(1)}, bf16[2,1024,704]{1,2,0:T(8,128)(2,1)}, u32[]{:S(2)}) copy-start(bf16[2,1024,704]{1,2,0:T(8,128)(2,1)} %param.26) | copy-start | bytes 8650756
  97.3 6.1 %copy-start.60 = (bf16[2,640,704]{1,2,0:T(8,128)(2,1)}, bf16[2,640,704]{1,2,0:T(8,128)(2,1)S(1)}, u32[]{:S(2)}) copy-start(bf16[2,640,704]{1,2,0:T(8,128)(2,1)S(1)} %get-tuple-element.81) | copy-start | bytes 5406724
  154.7 3.7 %copy-start.30 = (f32[1024,16]{0,1:T(8,128)S(1)}, f32[1024,16]{0,1:T(8,128)}, u32[]{:S(2)}) copy-start(f32[1024,16]{0,1:T(8,128)} %param.25) | copy-start | bytes 196612
  154.8 4.3 %copy-start.16 = (bf16[1,2,8,40,1024]{4,3,2,1,0:T(8,128)(2,1)S(1)}, bf16[1,2,8,40,1024]{4,3,2,1,0:T(8,128)(2,1)}, u32[]{:S(2)}) copy-start(bf16[1,2,8,40,1024]{4,3,2,1,0:T(8,128)(2,1)} %get-tuple-element.82) | copy-start | bytes 3932164
  162.8 3.1 copy-start.19
  162.8 3.0 copy-start.31
  166.2 10.8 %copy-start.23 = (bf16[128,1024]{0,1:T(8,128)(2,1)S(1)}, bf16[128,1024]{0,1:T(8,128)(2,1)}, u32[]{:S(2)}) copy-start(bf16[128,1024]{0,1:T(8,128)(2,1)} %copy-done.22) | copy-start | bytes 786436
  166.3 11.2 %copy-start.24 = (bf16[128,1024]{0,1:T(8,128)(2,1)S(1)}, bf16[128,1024]{0,1:T(8,128)(2,1)}, u32[]{:S(2)}) copy-start(bf16[128,1024]{0,1:T(8,128)(2,1)} %copy.75) | copy-start | bytes 786436
  166.3 11.5 %copy-start.12 = (bf16[1024,1024]{1,0:T(8,128)(2,1)S(1)}, bf16[1024,1024]{1,0:T(8,128)(2,1)}, u32[]{:S(2)}) copy-start(bf16[1024,1024]{1,0:T(8,128)(2,1)} %param.19) | copy-start | bytes 6291460
  180.8 3.4 %copy-start.32 = (f32[16,1024]{1,0:T(8,128)S(1)}, f32[16,1024]{1,0:T(8,128)}, u32[]{:S(2)}) copy-start(f32[16,1024]{1,0:T(8,128)} %fusion.29) | copy-start | bytes 196612
  180.8 3.4 %copy-start.36 = (f32[1024]{0:T(1024)S(1)}, f32[1024]{0:T(1024)}, u32[]{:S(2)}) copy-start(f32[1024]{0:T(1024)} %get-tuple-element.62) | copy-start | bytes 12292
  182.9 3.4 %copy-start.26 = (bf16[1,128,1024]{2,1,0:T(8,128)(2,1)S(1)}, bf16[1,128,1024]{2,1,0:T(8,128)(2,1)}, u32[]{:S(2)}) copy-start(bf16[1,128,1024]{2,1,0:T(8,128)(2,1)} %get-tuple-element.70) | copy-start | bytes 786436
  182.9 4.5 %copy-start.27 = (bf16[16,64,128]{2,1,0:T(8,128)(2,1)S(1)}, bf16[16,64,128]{2,1,0:T(8,128)(2,1)}, u32[]{:S(2)}) copy-start(bf16[16,64,128]{2,1,0:T(8,128)(2,1)} %convolution_convert_fusion.5) | copy-start | bytes 786436
  182.9 4.7 %copy-start.25 = (bf16[1,1024,128]{1,2,0:T(8,128)(2,1)S(1)}, bf16[1,1024,128]{1,2,0:T(8,128)(2,1)}, u32[]{:S(2)}) copy-start(bf16[1,1024,128]{1,2,0:T(8,128)(2,1)} %get-tuple-element.85) | copy-start | bytes 786436
  294.5 10.2 %copy-start.35 = (f32[32,1024]{1,0:T(8,128)S(1)}, f32[32,1024]{1,0:T(8,128)}, u32[]{:S(2)}) copy-start(f32[32,1024]{1,0:T(8,128)} %get-tuple-element.21) | copy-start | bytes 393220
  306.8 7.4 %copy-start.53 = (f32[128]{0:T(128)S(1)}, f32[128]{0:T(128)}, u32[]{:S(2)}) copy-start(f32[128]{0:T(128)} %get-tuple-element.65) | copy-start | bytes 1540
  306.8 7.4 %copy-start.18 = (f32[128,1024]{1,0:T(8,128)S(1)}, f32[128,1024]{1,0:T(8,128)}, u32[]{:S(2)}) copy-start(f32[128,1024]{1,0:T(8,128)} %copy-done.17) | copy-start | bytes 1572868
  306.8 8.4 %copy-start.6 = (bf16[2,2,8,40,1024]{4,3,2,1,0:T(8,128)(2,1)S(1)}, bf16[2,2,8,40,1024]{4,3,2,1,0:T(8,128)(2,1)}, u32[]{:S(2)}) copy-start(bf16[2,2,8,40,1024]{4,3,2,1,0:T(8,128)(2,1)} %copy-done.4) | copy-start | bytes 7864324
  306.8 8.4 %copy-start.59 = (bf16[2,640,704]{1,2,0:T(8,128)(2,1)S(1)}, bf16[2,640,704]{1,2,0:T(8,128)(2,1)}, u32[]{:S(2)}) copy-start(bf16[2,640,704]{1,2,0:T(8,128)(2,1)} %copy-done.58) | copy-start | bytes 5406724
  315.2 4.9 %copy-start.57 = (bf16[2,640,704]{1,2,0:T(8,128)(2,1)S(1)}, bf16[2,640,704]{1,2,0:T(8,128)(2,1)}, u32[]{:S(2)}) copy-start(bf16[2,640,704]{1,2,0:T(8,128)(2,1)} %copy-done.56) | copy-start | bytes 5406724
  320.1 4.9 %copy-start.1 = (bf16[2,704,1024]{2,1,0:T(8,128)(2,1)S(1)}, bf16[2,704,1024]{2,1,0:T(8,128)(2,1)}, u32[]{:S(2)}) copy-start(bf16[2,704,1024]{2,1,0:T(8,128)(2,1)} %param.28) | copy-start | bytes 8650756
  (29 other events, 52.2 us)

commit v2 on v1

--- a/solution.py
+++ b/solution.py
@@ -66,9 +66,12 @@
     for k in range(1, me.n_expert):
         to = (me.e + k) % me.n_expert
         copies.append(
-            remote(rows.at[to], recv.at[me.c, me.y, me.e], send_sem.at[k], recv_sem.at[k], me.at(e=to))
+            remote(
+                rows.at[to], recv.at[me.c, me.y * me.n_expert + me.e],
+                send_sem.at[k], recv_sem.at[k], me.at(e=to),
+            )
         )
-    recv[me.c, me.y, me.e] = rows[me.e]
+    recv[me.c, me.y * me.n_expert + me.e] = rows[me.e]
     return copies
 
 
@@ -78,12 +81,12 @@
         src = (me.e - k + me.n_expert) % me.n_expert
         if k:
             came[k - 1].wait_recv()
-        block = recv.at[me.c, me.y, src]
+        block = recv.at[me.c, me.y * me.n_expert + src]
         for s in range(1, me.ny):
             along_y.append(
                 remote(block, block, sy.at[s - 1, k], ry.at[s - 1, k], me.at(y=(me.y + s) % me.ny))
             )
-    block = recv.at[me.c, me.y]
+    block = recv.at[me.c, pl.ds(me.y * me.n_expert, me.n_expert)]
     across = [remote(block, block, sc.at[0], rc.at[0], me.at(c=1 - me.c))]
     return along_y, across
 
@@ -92,7 +95,8 @@
     for copy in along_y:
         copy.wait_recv()
     for s in range(1, me.ny):
-        block = recv.at[me.c, (me.y - s + me.ny) % me.ny]
+        column = (me.y - s + me.ny) % me.ny * me.n_expert
+        block = recv.at[me.c, pl.ds(column, me.n_expert)]
         across.append(remote(block, block, sc.at[s], rc.at[s], me.at(c=1 - me.c)))
 
 
@@ -173,7 +177,8 @@
     n_expert, n_dp = sizes
     ny, per_core = n_dp // 2, micro * cap
     seq, width = cot.shape
-    block = (2, ny, n_expert, 2 * per_core)
+    block = (2, ny * n_expert, 2 * per_core)
+    mine = (n_expert, 2 * per_core)
     bf = jnp.bfloat16
     return pl.pallas_call(
         functools.partial(spread_kernel, sizes, (micro, cap, per_core)),
@@ -188,9 +193,9 @@
             pltpu.VMEM((2,) + info.shape, jnp.int32),
             pltpu.VMEM((2, 2, seq, width), bf),
             pltpu.VMEM((2, 2, seq, 128), bf),
-            pltpu.VMEM(block[2:] + (width,), bf),
-            pltpu.VMEM(block[2:] + (width,), bf),
-            pltpu.VMEM(block[2:] + (128,), bf),
+            pltpu.VMEM(mine + (width,), bf),
+            pltpu.VMEM(mine + (width,), bf),
+            pltpu.VMEM(mine + (128,), bf),
             DMA((4,)),
             DMA((4,)),
             DMA((3, n_expert)),
@@ -207,85 +212,114 @@
     )(info, cot, moe, weights)
 
 
-def gather_back_kernel(sizes, p0_ref, p1_ref, q_out, r1, stage, r2, final, s1, t1, s2, t2, s3, t3, s4, t4):
+class Back:
+    def __init__(self, me, away, own, q_out, r1, stage, r2, final, sems):
+        self.me, self.away, self.own = me, away, own
+        self.q_out, self.r1, self.stage, self.r2, self.final = q_out, r1, stage, r2, final
+        self.sems = sems
+        self.ys = [(me.y + k) % me.ny for k in range(me.ny)]
+        self.order = list(range(1, me.n_expert)) + [0]
+        self.first, self.second, self.third, self.fourth = {}, {}, {}, {}
+
+    def to_mate(self, i):
+        s, r = self.sems[0].at[i], self.sems[1].at[i]
+        self.first[i] = remote(self.away(i), self.r1.at[i], s, r, self.me.at(c=1 - self.me.c))
+
+    def partial(self, i, y, e):
+        block = y * self.me.n_expert + e
+        return self.own(i, block) + self.r1[i, block].astype(jnp.float32)
+
+    def along_y(self, i):
+        me = self.me
+        self.first[i].wait_recv()
+        for k in range(1, me.ny):
+            for j in self.order:
+                e = (me.e + j) % me.n_expert
+                self.stage[i, k - 1, e] = self.partial(i, self.ys[k], e).astype(jnp.bfloat16)
+                self.second[i, k, j] = remote(
+                    self.stage.at[i, k - 1, e], self.r2.at[i, k - 1, e],
+                    self.sems[2].at[i, k - 1, j], self.sems[3].at[i, k - 1, j], me.at(y=self.ys[k]),
+                )
+
+    def finish(self, i, order):
+        me = self.me
+        for j in order:
+            e = (me.e + j) % me.n_expert
+            total = self.partial(i, me.y, e)
+            for k in range(1, me.ny):
+                self.second[i, k, j].wait_recv()
+                total = total + self.r2[i, k - 1, e].astype(jnp.float32)
+            if j:
+                self.final[i, e] = total.astype(jnp.bfloat16)
+                self.third[i, j] = remote(
+                    self.final.at[i, e], self.q_out.at[i, me.c, me.e],
+                    self.sems[4].at[i, j], self.sems[5].at[i, j], me.at(e=e),
+                )
+            else:
+                self.q_out[i, me.c, me.e] = total.astype(jnp.bfloat16)
+
+    def across(self, i):
+        for j in self.order[:-1]:
+            self.third[i, j].wait_recv()
+        block = self.q_out.at[i, self.me.c]
+        s, r = self.sems[6].at[i], self.sems[7].at[i]
+        self.fourth[i] = remote(block, block, s, r, self.me.at(c=1 - self.me.c))
+
+    def close(self):
+        for copy in self.fourth.values():
+            copy.wait()
+        for copies in (self.first, self.second, self.third):
+            for copy in copies.values():
+                copy.wait_send()
+
+
+def back_scratch(sizes, size, width):
+    n_expert, ny = sizes[0], sizes[1] // 2
+    most = max(ny - 1, 1)
+    bf = jnp.bfloat16
+    return [
+        pltpu.VMEM((2, ny * n_expert, size, width), bf),
+        pltpu.VMEM((2, most, n_expert, size, width), bf),
+        pltpu.VMEM((2, most, n_expert, size, width), bf),
+        pltpu.VMEM((2, n_expert, size, width), bf),
+        DMA((2,)),
+        DMA((2,)),
+        DMA((2, most, n_expert)),
+        DMA((2, most, n_expert)),
+        DMA((2, n_expert)),
+        DMA((2, n_expert)),
+        DMA((2,)),
+        DMA((2,)),
+    ]
+
+
+def gather_back_kernel(sizes, p0_ref, p1_ref, q_out, *scratch):
     me = Place(*sizes)
     greet(column_peers(me))
-    c, mate = me.c, me.at(c=1 - me.c)
     p_refs = (p0_ref, p1_ref)
-    count = 2
-    ys = [(me.y + k) % me.ny for k in range(me.ny)]
-    order = list(range(1, me.n_expert)) + [0]
-    first = {}
-    for i in range(count):
-        for k in list(range(1, me.ny)) + [0]:
-            y = ys[k]
-            first[i, k] = remote(
-                p_refs[i].at[1 - c, y], r1.at[i, y], s1.at[i, k], t1.at[i, k], mate
-            )
-    second, third, fourth = {}, {}, []
-    for i in range(count):
-        for k in range(1, me.ny):
-            first[i, k].wait_recv()
-            for j in order:
-                e = (me.e + j) % me.n_expert
-                total = p_refs[i][c, ys[k], e].astype(jnp.float32) + r1[i, ys[k], e].astype(jnp.float32)
-                stage[i, k - 1, e] = total.astype(jnp.bfloat16)
-                second[i, k, j] = remote(
-                    stage.at[i, k - 1, e], r2.at[i, k - 1, e], s2.at[i, k - 1, j], t2.at[i, k - 1, j],
-                    me.at(y=ys[k]),
-                )
-    for i in range(count):
-        first[i, 0].wait_recv()
-        for j in order:
-            e = (me.e + j) % me.n_expert
-            total = p_refs[i][c, me.y, e].astype(jnp.float32) + r1[i, me.y, e].astype(jnp.float32)
-            for k in range(1, me.ny):
-                second[i, k, j].wait_recv()
-                total = total + r2[i, k - 1, e].astype(jnp.float32)
-            if j:
-                final[i, e] = total.astype(jnp.bfloat16)
-                third[i, j] = remote(
-                    final.at[i, e], q_out.at[i, c, me.e], s3.at[i, j], t3.at[i, j], me.at(e=e)
-                )
-            else:
-                q_out[i, c, me.e] = total.astype(jnp.bfloat16)
-    for i in range(count):
-        for j in order[:-1]:
-            third[i, j].wait_recv()
-        block = q_out.at[i, c]
-        fourth.append(remote(block, block, s4.at[i], t4.at[i], mate))
-    for copy in fourth:
-        copy.wait()
-    for copies in (first, second, third):
-        for copy in copies.values():
-            copy.wait_send()
+    back = Back(
+        me, lambda i: p_refs[i].at[1 - me.c],
+        lambda i, block: p_refs[i][me.c, block].astype(jnp.float32), q_out, *scratch[:4], scratch[4:],
+    )
+    for i in range(2):
+        back.to_mate(i)
+    for i in range(2):
+        back.along_y(i)
+    for i in range(2):
+        back.finish(i, back.order)
+        back.across(i)
+    back.close()
 
 
 def gather_back(sizes, first, second):
-    n_expert, n_dp = sizes
-    count = 2
-    _, ny, _, rows, width = first.shape
-    bf = jnp.bfloat16
-    most = max(ny - 1, 1)
+    n_expert = sizes[0]
+    _, _, size, width = first.shape
     return pl.pallas_call(
         functools.partial(gather_back_kernel, sizes),
-        out_shape=jax.ShapeDtypeStruct((count, 2, n_expert, rows, width), bf),
+        out_shape=jax.ShapeDtypeStruct((2, 2, n_expert, size, width), jnp.bfloat16),
         in_specs=[VMEM] * 2,
         out_specs=VMEM,
-        scratch_shapes=[
-            pltpu.VMEM((count, ny, n_expert, rows, width), bf),
-            pltpu.VMEM((count, most, n_expert, rows, width), bf),
-            pltpu.VMEM((count, most, n_expert, rows, width), bf),
-            pltpu.VMEM((count, n_expert, rows, width), bf),
-            DMA((count, ny)),
-            DMA((count, ny)),
-            DMA((count, most, n_expert)),
-            DMA((count, most, n_expert)),
-            DMA((count, n_expert)),
-            DMA((count, n_expert)),
-            DMA((count,)),
-            DMA((count,)),
-        ],
+        scratch_shapes=back_scratch(sizes, size, width),
         name="gather_back",
         compiler_params=pltpu.CompilerParams(
             collective_id=2, has_side_effects=True, vmem_limit_bytes=48 << 20
@@ -293,10 +327,152 @@
     )(first, second)
 
 
+def gated_terms(gate_pre, up_pre):
+    root = math.sqrt(2.0 / math.pi)
+    square = gate_pre * gate_pre
+    bend = jnp.tanh(root * (gate_pre + 0.044715 * square * gate_pre))
+    half = 0.5 * (1.0 + bend)
+    active = gate_pre * half
+    slope = half + 0.5 * gate_pre * (1.0 - bend * bend) * root * (1.0 + 3 * 0.044715 * square)
+    return active * up_pre, active, up_pre * slope
+
+
+def expert_kernel(
+    sizes, x_ref, g_ref, w_ref, wg_hbm, wu_hbm, wd_hbm,
+    q_out, hid_out, dg_out, du_out, gr_out,
+    wg, wu, wd, act, slope, away, own, sem_w, *scratch,
+):
+    me = Place(*sizes)
+    c = me.c
+    fetch = {}
+    for n, j in enumerate((1 - c, c)):
+        for i, (src, dst) in enumerate(((wg_hbm, wg), (wu_hbm, wu), (wd_hbm, wd))):
+            fetch[n, i] = pltpu.make_async_copy(src.at[j], dst.at[j], sem_w.at[n, i])
+            fetch[n, i].start()
+    greet(column_peers(me))
+    bf, f32 = jnp.bfloat16, jnp.float32
+    size = x_ref.shape[2]
+    column = me.n_expert
+    half = column // 2
+    step = math.gcd(column, 4)
+    chunk = step * size
+    back = Back(
+        me, lambda i: away.at[i],
+        lambda i, block: own[i, pl.ds(pl.multiple_of(block * size, 8), size), :],
+        q_out, *scratch[:4], scratch[4:],
+    )
+
+    def dot(left, right, contract):
+        return lax.dot_general(left, right, (contract, ((), ())), preferred_element_type=f32)
+
+    def flat(value):
+        return value.reshape(chunk, value.shape[-1])
+
+    def blocks(value):
+        return value.reshape(step, size, value.shape[-1])
+
+    def store(i, first, some, rows, value):
+        if first:
+            away[i, some] = blocks(value.astype(bf))
+        else:
+            own[i, rows, :] = value
+
+    def each(start, count, body):
+        @pl.loop(0, count // step)
+        def _(n):
+            at = start + n * step
+            body(pl.ds(at, step), pl.ds(pl.multiple_of(at * size, 8), chunk))
+
+    def forward(first, j, start, count):
+        def body(some, rows):
+            x = flat(x_ref[j, some])
+            gate_pre = dot(x, wg[j], ((1,), (0,)))
+            up_pre = dot(x, wu[j], ((1,), (0,)))
+            hidden, active, lean = gated_terms(gate_pre, up_pre)
+            act[j, rows, :] = active
+            slope[j, rows, :] = lean
+            hidden = hidden.astype(bf)
+            hid_out[j, some] = blocks(hidden)
+            store(0, first, some, rows, dot(hidden, wd[j], ((1,), (0,))))
+
+        each(start, count, body)
+
+    def backward(first, j, start, count):
+        def body(some, rows):
+            pieces = flat(w_ref[j, some].astype(f32))
+            weight = pieces[:, 0:1] + pieces[:, 1:2] + pieces[:, 2:3]
+            grad = (weight * flat(g_ref[j, some].astype(f32))).astype(bf)
+            gr_out[j, some] = blocks(grad)
+            grad_hidden = dot(grad, wd[j], ((1,), (1,)))
+            dg = (grad_hidden * slope[j, rows, :]).astype(bf)
+            du = (grad_hidden * act[j, rows, :]).astype(bf)
+            dg_out[j, some] = blocks(dg)
+            du_out[j, some] = blocks(du)
+            store(1, first, some, rows, dot(dg, wg[j], ((1,), (1,))) + dot(du, wu[j], ((1,), (1,))))
+
+        each(start, count, body)
+
+    for i in range(3):
+        fetch[0, i].wait()
+    forward(True, 1 - c, 0, me.ny * column)
+    back.to_mate(0)
+    for i in range(3):
+        fetch[1, i].wait()
+    for k in range(1, me.ny):
+        forward(False, c, back.ys[k] * column, column)
+    back.along_y(0)
+    forward(False, c, me.y * column, column)
+    backward(True, 1 - c, 0, me.ny * column)
+    back.to_mate(1)
+    back.finish(0, back.order[:half])
+    for k in range(1, me.ny):
+        backward(False, c, back.ys[k] * column, column)
+    back.along_y(1)
+    backward(False, c, me.y * column, column)
+    back.finish(0, back.order[half:])
+    back.across(0)
+    back.finish(1, back.order)
+    back.across(1)
+    back.close()
+
+
+def experts(sizes, x, g, w, w_gate, w_up, w_down):
+    n_expert = sizes[0]
+    _, count, size, width = x.shape
+    units = w_gate.shape[2]
+    bf, f32 = jnp.bfloat16, jnp.float32
+    any_space = pl.BlockSpec(memory_space=pl.ANY)
+    inner = jax.ShapeDtypeStruct((2, count, size, units), bf)
+    return pl.pallas_call(
+        functools.partial(expert_kernel, sizes),
+        out_shape=(
+            jax.ShapeDtypeStruct((2, 2, n_expert, size, width), bf),
+            inner, inner, inner,
+            jax.ShapeDtypeStruct(x.shape, bf),
+        ),
+        in_specs=[VMEM] * 3 + [any_space] * 3,
+        out_specs=(VMEM,) * 5,
+        scratch_shapes=[
+            pltpu.VMEM(w_gate.shape, bf),
+            pltpu.VMEM(w_up.shape, bf),
+            pltpu.VMEM(w_down.shape, bf),
+            pltpu.VMEM((2, count * size, units), f32),
+            pltpu.VMEM((2, count * size, units), f32),
+            pltpu.VMEM((2, count, size, width), bf),
+            pltpu.VMEM((2, count * size, width), f32),
+            DMA((2, 3)),
+        ]
+        + back_scratch(sizes, size, width),
+        name="experts",
+        compiler_params=pltpu.CompilerParams(
+            collective_id=4, has_side_effects=True, vmem_limit_bytes=60 << 20
+        ),
+    )(x, g, w, w_gate, w_up, w_down)
+
+
 def reduce_kernel(
     sizes, pieces, left_ref, right_ref, small_ref, out, small_out,
-    buf_a, buf_b, acc, part0, part1, part2, got0, got1, got2, half, small_half, small_got,
-    fs, fr, os, ps, pr, gs, gr, ms, mr, cs, cr, ss, sr,
+    buf_a, buf_b, acc, *boxes,
 ):
     me = Place(*sizes)
     c, mate = me.c, me.at(c=1 - me.c)
@@ -315,9 +491,11 @@
     dims = [
         (n, other, lambda q: along(pair, q)),
         (nh, hi, lambda q: along(q * 2 + lo, other)),
-        (me.nz, me.z, lambda q: me.at(z=q)),
+        (2, me.z % 2, lambda q: me.at(z=me.z // 2 * 2 + q)),
+        (me.nz // 2, me.z // 2, lambda q: me.at(z=q * 2 + me.z % 2)),
     ]
-    parts, gots = [part0, part1, part2], [got0, got1, got2]
+    parts, gots = boxes[:4], boxes[4:8]
+    half, small_half, small_got, fs, fr, os, ps, pr, gs, gr, ms, mr, cs, cr, ss, sr = boxes[8:]
     levels = [i for i, d in enumerate(dims) if d[0] > 1]
     x_peers = [me.at(x=(me.x + k) % n) for k in range(1, n)]
     y_peers = [me.at(y=(me.y + k) % n) for k in range(1, n)]
@@ -327,7 +505,7 @@
     )
 
     def slot_a(slot):
-        return buf_a.at[:, pl.ds(pl.multiple_of(slot * seq, seq), seq)]
+        return buf_a.at[pl.ds(pl.multiple_of(slot * seq, seq), seq), :]
 
     def slot_b(slot):
         return buf_b.at[pl.ds(pl.multiple_of(slot * seq, seq), seq), :]
@@ -350,37 +528,44 @@
         copy.start()
     rows_s = half.shape[0]
     small = [remote(small_ref.at[pl.ds((1 - c) * rows_s, rows_s)], half, ss.at[0], sr.at[0], mate)]
-    small[0].wait_recv()
-    small_half[0] = small_ref[pl.ds(c * rows_s, rows_s)] + half[...]
-    slot = 1
-    for level, (count, index, peer) in enumerate(
-        ((n, me.x, lambda q: me.at(x=q)), (n, me.y, lambda q: me.at(y=q)), (me.nz, me.z, lambda q: me.at(z=q)))
-    ):
-        if count > 1:
-            copies = []
+    small_dims = [
+        (n, me.x, lambda q: me.at(x=q)),
+        (n, me.y, lambda q: me.at(y=q)),
+        (me.nz, me.z, lambda q: me.at(z=q)),
+    ]
+    small_wait = [small[0]]
+    small_slot = [1]
+
+    def small_step(step):
+        for copy in small_wait:
+            copy.wait_recv()
+        small_wait.clear()
+        if step == 0:
+            total = small_ref[pl.ds(c * rows_s, rows_s)] + half[...]
+        elif step <= 3:
+            total = small_got[step - 1, 0]
+            for k in range(1, small_dims[step - 1][0]):
+                total = total + small_got[step - 1, k]
+        if step < 3:
+            count, index, peer = small_dims[step]
+            small_half[step] = total
+            small_got[step, index] = total
             for k in range(1, count):
-                copies.append(
+                small_wait.append(
                     remote(
-                        small_half.at[level], small_got.at[level, index], ss.at[slot], sr.at[slot],
-                        peer((index + k) % count),
+                        small_half.at[step], small_got.at[step, index], ss.at[small_slot[0]],
+                        sr.at[small_slot[0]], peer((index + k) % count),
                     )
                 )
-                slot += 1
-            small_got[level, index] = small_half[level]
-            for copy in copies:
-                copy.wait_recv()
-            small += copies
-            total = small_got[level, 0]
-            for k in range(1, count):
-                total = total + small_got[level, k]
-        else:
-            total = small_half[level]
-        if level < 2:
-            small_half[level + 1] = total
-        else:
+                small_slot[0] += 1
+        elif step == 3:
             small_out[pl.ds(c * rows_s, rows_s)] = total
-    block = small_out.at[pl.ds(c * rows_s, rows_s)]
-    small.append(remote(block, block, ss.at[slot], sr.at[slot], mate))
+            block = small_out.at[pl.ds(c * rows_s, rows_s)]
+            small_wait.append(
+                remote(block, block, ss.at[small_slot[0]], sr.at[small_slot[0]], mate)
+            )
+        small.extend(small_wait)
+
     for where in (1 - c, 2, 3):
         for i, (src, dst) in enumerate(((left_ref, slot_a(where)), (right_ref, slot_b(where)))):
             pltpu.make_async_remote_copy(
@@ -395,8 +580,9 @@
     pending = {}
 
     def multiply(k):
-        acc[k] = jnp.dot(
-            buf_a[k * rows_k : (k + 1) * rows_k, :], buf_b[...], preferred_element_type=jnp.float32
+        acc[k] = lax.dot_general(
+            buf_a[:, k * rows_k : (k + 1) * rows_k], buf_b[...], (((0,), (0,)), ((), ())),
+            preferred_element_type=jnp.float32,
         )
         push(k, 0, rows_k)
 
@@ -475,12 +661,17 @@
     steps = [multiply]
     steps += [functools.partial(add, at=i) for i in range(len(levels))]
     steps += [functools.partial(shared, at=i) for i in reversed(range(len(levels)))]
-    steps += [across, lambda k: pending["core", k].wait_recv()]
-    for t in range(pieces + len(steps) - 1):
-        for p in reversed(range(len(steps))):
-            if 0 <= t - p < pieces:
-                steps[p](t - p)
-    small[-1].wait_recv()
+    events = sorted((0 if p == 0 else p + k, -p, k) for p in range(len(steps)) for k in range(pieces))
+    before = 0
+    for t, p, k in events:
+        if before < t <= 5:
+            small_step(t - 1)
+        before = t
+        steps[-p](k)
+    for k in range(pieces):
+        across(k)
+    for k in range(pieces):
+        pending["core", k].wait_recv()
     for copy in factor + small:
         copy.wait_send()
     for copies in pending.values():
@@ -488,19 +679,19 @@
             copy.wait_send()
 
 
-def reduce_all(sizes, left, right, small):
+def reduce_all(sizes, left, right, small, pieces=8):
     n_expert, n_dp = sizes
     nz = math.gcd(n_expert, 4)
     n = n_expert // nz
     nh = n // 2
     assert n == n_dp // 2
-    width, seq = left.shape[1:]
-    pieces = 4
+    seq, width = left.shape[1:]
     rows_k = width // pieces
     bf, f32 = jnp.bfloat16, jnp.float32
     rows_s = small.shape[0] // 2
-    sizes_at = [rows_k // n, rows_k // (n * nh), rows_k // (n * nh * nz)]
-    counts = [max(n - 1, 1), max(nh - 1, 1), max(nz - 1, 1)]
+    splits = [n, nh, 2, nz // 2]
+    sizes_at = [rows_k // math.prod(splits[: i + 1]) for i in range(4)]
+    counts = [max(q - 1, 1) for q in splits]
     most = max(counts)
     boxes = [pltpu.VMEM((pieces, q, s, width), bf) for q, s in zip(counts, sizes_at)]
     smalls = 2 * n + nz
@@ -513,7 +704,7 @@
         in_specs=[VMEM] * 3,
         out_specs=(VMEM, VMEM),
         scratch_shapes=[
-            pltpu.VMEM((width, 4 * seq), bf),
+            pltpu.VMEM((4 * seq, width), bf),
             pltpu.VMEM((4 * seq, width), bf),
             pltpu.VMEM((pieces, rows_k, width), f32),
             *boxes,
@@ -524,10 +715,10 @@
             DMA((3, 2)),
             DMA((4, 2)),
             DMA((2,)),
-            DMA((3, pieces, most)),
-            DMA((3, pieces, most)),
-            DMA((3, pieces, most)),
-            DMA((3, pieces, most)),
+            DMA((4, pieces, most)),
+            DMA((4, pieces, most)),
+            DMA((4, pieces, most)),
+            DMA((4, pieces, most)),
             DMA((pieces,)),
             DMA((pieces,)),
             DMA((pieces,)),
@@ -537,7 +728,7 @@
         ],
         name="reduce_all",
         compiler_params=pltpu.CompilerParams(
-            collective_id=3, has_side_effects=True, vmem_limit_bytes=56 << 20
+            collective_id=3, has_side_effects=True, vmem_limit_bytes=24 << 20
         ),
     )(left, right, small)
 
@@ -556,10 +747,6 @@
     bucketed = jnp.where(distance < 8, distance, far_bucket) + 16 * (relative > 0).astype(jnp.int32)
     bucket_ids = jnp.arange(buckets, dtype=jnp.int32)
     return (bucketed[None, :, :] == bucket_ids[:, None, None]).astype(jnp.float32)
-
-
-def gated_product(gate_pre, up_pre):
-    return jax.nn.gelu(gate_pre, approximate=True) * up_pre
 
 
 def dot32(pattern, left, right):
@@ -613,24 +800,32 @@
     grad_in, rows_in, weight_in = spread(
         sizes, MICRO, capacity, info, cotangent, moe_in.astype(bf), weights
     )
-    block = grad_in.shape[:-1]
-    expert_rows = rows_in.reshape(2, -1, width)
-    slot_weight = jnp.sum(weight_in[..., :3].astype(f32), axis=-1).reshape(2, -1, 1)
-    grad_rows = (slot_weight * grad_in.reshape(2, -1, width).astype(f32)).astype(bf)
-    gate_pre = dot32("jrd,jdf->jrf", expert_rows, w_gate)
-    up_pre = dot32("jrd,jdf->jrf", expert_rows, w_up)
-    product, pullback = jax.vjp(gated_product, gate_pre, up_pre)
-    hidden = product.astype(bf)
-    partial_out = dot32("jrf,jfd->jrd", hidden, w_down).astype(bf)
-    hidden_grad = dot32("jrd,jfd->jrf", grad_rows, w_down)
-    gate_grad, up_grad = [g.astype(bf) for g in pullback(hidden_grad)]
-    rows_grad = dot32("jrf,jdf->jrd", gate_grad, w_gate) + dot32("jrf,jdf->jrd", up_grad, w_up)
-    grad_w_gate = dot32("jrd,jrf->jdf", expert_rows, gate_grad)
-    grad_w_up = dot32("jrd,jrf->jdf", expert_rows, up_grad)
+    if 23 * rows_in.size + 6 * w_gate.size < 52 << 20:
+        back, hidden, gate_grad, up_grad, grad_rows = experts(
+            sizes, rows_in, grad_in, weight_in, w_gate, w_up, w_down
+        )
+    else:
+        blocks = rows_in.shape[:-1] + (-1,)
+        rows_in, grad_in, weight_in = [
+            a.reshape(2, -1, a.shape[-1]) for a in (rows_in, grad_in, weight_in)
+        ]
+        slot_weight = jnp.sum(weight_in[..., :3].astype(f32), axis=-1, keepdims=True)
+        grad_rows = (slot_weight * grad_in.astype(f32)).astype(bf)
+        gate_pre = dot32("jrd,jdf->jrf", rows_in, w_gate)
+        up_pre = dot32("jrd,jdf->jrf", rows_in, w_up)
+        hidden, active, lean = gated_terms(gate_pre, up_pre)
+        hidden = hidden.astype(bf)
+        partial_out = dot32("jrf,jfd->jrd", hidden, w_down).astype(bf)
+        hidden_grad = dot32("jrd,jfd->jrf", grad_rows, w_down)
+        gate_grad, up_grad = (hidden_grad * lean).astype(bf), (hidden_grad * active).astype(bf)
+        rows_grad = dot32("jrf,jdf->jrd", gate_grad, w_gate) + dot32("jrf,jdf->jrd", up_grad, w_up)
+        back = gather_back(sizes, partial_out.reshape(blocks), rows_grad.astype(bf).reshape(blocks))
+    rows_in, hidden, gate_grad, up_grad, grad_rows = [
+        a.reshape(2, -1, a.shape[-1]) for a in (rows_in, hidden, gate_grad, up_grad, grad_rows)
+    ]
+    grad_w_gate = dot32("jrd,jrf->jdf", rows_in, gate_grad)
+    grad_w_up = dot32("jrd,jrf->jdf", rows_in, up_grad)
     grad_w_down = dot32("jrf,jrd->jfd", hidden, grad_rows)
-    back = gather_back(
-        sizes, partial_out.reshape(block + (width,)), rows_grad.astype(bf).reshape(block + (width,))
-    )
     back = back.reshape(2, -1, width)
 
     core = lax.axis_index("dp") % 2
@@ -691,7 +886,7 @@
     small = jnp.pad(small, ((0, -small.shape[0] % 16), (0, 0)))
     sums, small = reduce_all(
         sizes,
-        jnp.stack([attn_in.T, context.T]),
+        jnp.stack([attn_in, context]),
         jnp.stack([grad_queries, grad_keys, grad_values, grad_attn_low]),
         small,
     )

time: 331 us -> 311 us (0.940); the launches traced: 325 us -> 310 us
  matrix products: 67.4 us -> 47.5 us
  other arithmetic: 34 us -> 17.3 us
  local copies, waits for them, and re-layouts: 20.4 us -> 34.9 us
  Pallas kernels: 202 us -> 209 us
    dot_general x26 -> x20, matrix products: 62.1 us -> 41.7 us  [dot32(): return jnp.einsum(pattern, left, right, preferred_element_type=jnp.float32)]
    unnamed x123 -> x111, local copies, waits for them, and re-layouts: 6.7 us -> 21.3 us
    pallas_call x1, Pallas kernels: 47.2 us -> 59.2 us  [experts(): pl.pallas_call(functools.partial(expert_kernel, sizes), out_shape=(jax.Sh...]
    mul x1, other arithmetic: 10.7 us -> 0.2 us  [shards(): probs * (grad_probs - jnp.sum(probs * grad_probs, axis=-1, keepdims=True))]
    pallas_call x1, Pallas kernels: 106 us -> 101 us  [reduce_all(): pl.pallas_call(functools.partial(reduce_kernel, sizes, pieces), out_shape...]
where the time goes in v2:
time: 311 us; the launch traced here: 310 us
  Pallas kernels  209 us (67%)
  matrix products  47.5 us (15%)
  local copies, waits for them, and re-layouts  34.9 us (11%)
  other arithmetic  17.3 us (6%)
    pallas_call x1, Pallas kernels, reduce_all(): pl.pallas_call(functools.partial(reduce_kernel, sizes, pieces), out_shape...  101 us
    pallas_call x1, Pallas kernels, experts(): pl.pallas_call(functools.partial(expert_kernel, sizes), out_shape=(jax.Sh...  59.2 us
    pallas_call x1, Pallas kernels, spread(): pl.pallas_call(functools.partial(spread_kernel, sizes, (micro, cap, per_c...  48.6 us
    dot_general x20, matrix products, dot32(): return jnp.einsum(pattern, left, right, preferred_element_type=jnp.float32)  41.7 us
    unnamed x111, local copies, waits for them, and re-layouts  21.3 us
    convert_element_type x1, other arithmetic, shards(): matrices = [sums[i].astype(f32) for i in range(4)]  10.2 us

profile of v2, /device:TPU:1, one launch (start us, length us, event | category | flops | bytes accessed | tf_op | source)
XLA Modules:
  0.0 310.0 jit_solution(4234693424461768387)
XLA Ops:
  0.7 1.2 fusion.18
  1.9 2.2 convolution_convert_fusion.7
  5.0 2.1 convolution_convert_fusion.6
  7.3 2.2 convolution_convert_fusion.5
  9.7 1.7 fusion.2
  11.5 2.5 copy.84
  14.0 1.6 convolution_add_fusion
  16.6 1.2 fusion.82
  18.4 1.9 convolution_convert_fusion.4
  23.9 48.6 %spread.1 = (bf16[2,16,40,1024]{3,2,1,0:T(8,128)(2,1)S(1)}, bf16[2,16,40,1024]{3,2,1,0:T(8,128)(2,1)S(1)}, bf16[2,16,40,128]{3,2,1,0:T(8,128)(2,1)S(1)}) custom-call(s32[8,128]{1,0:T(8,128)S(1)} %add_add_fusion.info_ref, bf16[128,1024]{1,0:T(8,128)(2,1)S(1)} %copy-done.6, bf16[128,1024]{1,0:T(8,128)(2,1)S(1)} %multiply_convert_fusion.moe_ref, ...), custom_call_target="tpu_custom_call" | custom-call | tf_op jit(solution)/shard_map/spread/pallas_call | solution.py:183
  72.6 1.5 copy-done.3
  74.1 1.5 copy-done.5
  76.3 4.6 %copy.87.wg_hbm = bf16[2,1024,704]{2,1,0:T(8,128)(2,1)} copy(bf16[2,1024,704]{1,2,0:T(8,128)(2,1)} %param.26) | data formatting | bytes 5767168 | tf_op args[11]
  80.9 4.6 %copy.88.wu_hbm = bf16[2,1024,704]{2,1,0:T(8,128)(2,1)} copy(bf16[2,1024,704]{1,2,0:T(8,128)(2,1)} %param.27) | data formatting | bytes 5767168 | tf_op args[12]
  85.5 59.2 %experts.1 = (bf16[2,2,8,40,1024]{4,3,2,1,0:T(8,128)(2,1)}, bf16[2,16,40,704]{3,2,1,0:T(8,128)(2,1)}, bf16[2,16,40,704]{3,2,1,0:T(8,128)(2,1)}, bf16[2,16,40,704...) custom-call(bf16[2,16,40,1024]{3,2,1,0:T(8,128)(2,1)} %copy-done.3, bf16[2,16,40,1024]{3,2,1,0:T(8,128)(2,1)} %copy-done.5, ...), custom_call_target="tpu_custom_call" | custom-call | tf_op jit(solution)/shard_map/experts/pallas_call | solution.py:446
  144.6 3.5 %fusion.80 = (bf16[1,2,8,40,1024]{4,3,2,1,0:T(8,128)(2,1)}, bf16[1,2,8,40,1024]{4,3,2,1,0:T(8,128)(2,1)}) fusion(bf16[2,2,8,40,1024]{4,3,2,1,0:T(8,128)(2,1)} %get-tuple-element.26), kind=kLoop, calls=%fused_computation.152 | loop fusion | bytes 5242880 | tf_op jit(solution)/shard_map/slice | solution.py:847
  148.3 1.9 fusion.28
  152.0 1.0 convert_bitcast_fusion
  154.9 1.7 multiply_reduce_fusion
  159.9 1.6 convolution_add_fusion.3
  161.5 3.0 convolution_convert_fusion
  164.5 2.0 convolution_add_fusion.2
  166.9 1.0 fusion.16
  169.3 1.1 pad_maximum_fusion.right_ref
  170.4 2.6 copy.97
  173.0 2.4 fusion.5
  176.0 101.0 %reduce_all.1 = (bf16[4,1024,1024]{2,1,0:T(8,128)(2,1)S(1)}, f32[32,1024]{1,0:T(8,128)S(1)}) custom-call(bf16[2,128,1024]{2,1,0:T(8,128)(2,1)S(1)} %pad_maximum_fusion.1.left_ref, bf16[4,128,1024]{2,1,0:T(8,128)(2,1)S(1)} %pad_maximum_fusion.right_ref, f32[32,1024]{1,0:T(8,128)S(1)} %select_maximum_fusion.small_ref), custom_call_target="tpu_custom_call" | custom-call | tf_op jit(solution)/shard_map/reduce_all/pallas_call | solution.py:698
  277.0 3.2 %copy-done.2 = bf16[4,1024,1024]{2,1,0:T(8,128)(2,1)} copy-done((bf16[4,1024,1024]{2,1,0:T(8,128)(2,1)}, bf16[4,1024,1024]{2,1,0:T(8,128)(2,1)S(1)}, u32[]{:S(2)}) %copy-start.2) | copy-done | bytes 8388632
  280.9 10.2 %bitcast_convert_fusion = (f32[1024,1024]{1,0:T(8,128)}, f32[1024,1024]{1,0:T(8,128)}, f32[1024,1024]{1,0:T(8,128)}, f32[1024,1024]{1,0:T(8,128)}) fusion(bf16[4,1024,1024]{2,1,0:T(8,128)(2,1)} %copy-done.2), kind=kLoop, calls=%fused_computation.1 | loop fusion | flops 4194304 | bytes 25165824 | tf_op jit(solution)/shard_map/convert_element_type | solution.py:893
  292.4 7.5 %fusion.85 = f32[2,1024,704]{1,2,0:T(8,128)} fusion(bf16[2,640,1024]{2,1,0:T(8,128)(2,1)} %bitcast.112, bf16[2,640,704]{2,1,0:T(8,128)(2,1)} %bitcast.143), kind=kOutput, calls=%fused_computation.157 | convolution fusion | flops 1845493760 | bytes 10190848 | tf_op jit(solution)/shard_map/jrd,jrf->jdf/dot_general | solution.py:753
  299.9 5.0 %fusion.86 = f32[2,1024,704]{1,2,0:T(8,128)} fusion(bf16[2,640,1024]{2,1,0:T(8,128)(2,1)S(1)} %bitcast.113, bf16[2,640,704]{2,1,0:T(8,128)(2,1)S(1)} %bitcast.142), kind=kOutput, calls=%fused_computation.158 | convolution fusion | flops 1845493760 | bytes 10190848 | tf_op jit(solution)/shard_map/jrd,jrf->jdf/dot_general | solution.py:753
  304.9 5.0 %fusion.87 = f32[2,704,1024]{2,1,0:T(8,128)} fusion(bf16[2,640,704]{2,1,0:T(8,128)(2,1)S(1)} %bitcast.141, bf16[2,640,1024]{2,1,0:T(8,128)(2,1)S(1)} %bitcast.140), kind=kOutput, calls=%fused_computation.159 | convolution fusion | flops 1845493760 | bytes 10190848 | tf_op jit(solution)/shard_map/jrf,jrd->jfd/dot_general | solution.py:753
  (154 shorter events, 18.2 us)
Async XLA Ops:
  0.6 19.8 %copy-start = (bf16[1024,1024]{1,0:T(8,128)(2,1)S(1)}, bf16[1024,1024]{1,0:T(8,128)(2,1)}, u32[]{:S(2)}) copy-start(bf16[1024,1024]{1,0:T(8,128)(2,1)} %param.22) | copy-start | bytes 6291460
  0.7 4.3 %copy-start.9 = (bf16[128,1024]{1,0:T(8,128)(2,1)S(1)}, bf16[128,1024]{1,0:T(8,128)(2,1)}, u32[]{:S(2)}) copy-start(bf16[128,1024]{1,0:T(8,128)(2,1)} %param.15) | copy-start | bytes 786436
  0.7 4.3 %copy-start.32 = (f32[1024]{0:T(1024)S(1)}, f32[1024]{0:T(1024)}, u32[]{:S(2)}) copy-start(f32[1024]{0:T(1024)} %param.18) | copy-start | bytes 12292
  1.9 5.3 %copy-start.36 = (f32[128]{0:T(128)}, f32[128]{0:T(128)S(1)}, u32[]{:S(2)}) copy-start(f32[128]{0:T(128)S(1)} %add_rsqrt_fusion.1) | copy-start | bytes 1540
  7.1 2.7 copy-start.40
  7.3 6.8 %copy-start.19 = (bf16[128,1024]{0,1:T(8,128)(2,1)}, bf16[128,1024]{0,1:T(8,128)(2,1)S(1)}, u32[]{:S(2)}) copy-start(bf16[128,1024]{0,1:T(8,128)(2,1)S(1)} %copy.82) | copy-start | bytes 786436
  9.6 6.0 %copy-start.21 = (bf16[128,1024]{0,1:T(8,128)(2,1)}, bf16[128,1024]{0,1:T(8,128)(2,1)S(1)}, u32[]{:S(2)}) copy-start(bf16[128,1024]{0,1:T(8,128)(2,1)S(1)} %copy.83) | copy-start | bytes 786436
  14.0 4.4 %copy-start.29 = (bf16[128,1024]{0,1:T(8,128)(2,1)S(1)}, bf16[128,1024]{0,1:T(8,128)(2,1)}, u32[]{:S(2)}) copy-start(bf16[128,1024]{0,1:T(8,128)(2,1)} %copy.81) | copy-start | bytes 786436
  20.4 3.5 %copy-start.6 = (bf16[128,1024]{1,0:T(8,128)(2,1)S(1)}, bf16[128,1024]{1,0:T(8,128)(2,1)}, u32[]{:S(2)}) copy-start(bf16[128,1024]{1,0:T(8,128)(2,1)} %cot_ref.1) | copy-start | bytes 786436
  144.6 3.5 %copy-start.39 = (s32[128,2]{0,1:T(2,128)S(1)}, s32[128,2]{0,1:T(2,128)}, u32[]{:S(2)}) copy-start(s32[128,2]{0,1:T(2,128)} %param.16) | copy-start | bytes 3076
  144.6 3.5 %copy-start.50 = (s32[128,2]{0,1:T(2,128)S(1)}, s32[128,2]{0,1:T(2,128)}, u32[]{:S(2)}) copy-start(s32[128,2]{0,1:T(2,128)} %param.17) | copy-start | bytes 3076
  148.2 2.0 copy-start.10
  148.2 2.5 copy-start.46
  148.2 2.5 copy-start.48
  148.2 2.5 copy-start.28
  148.2 2.5 copy-start.42
  148.3 2.5 copy-start.44
  148.3 3.1 %copy-start.14 = (bf16[1,2,8,40,1024]{4,3,2,1,0:T(8,128)(2,1)S(1)}, bf16[1,2,8,40,1024]{4,3,2,1,0:T(8,128)(2,1)}, u32[]{:S(2)}) copy-start(bf16[1,2,8,40,1024]{4,3,2,1,0:T(8,128)(2,1)} %get-tuple-element.89) | copy-start | bytes 3932164
  153.0 1.8 copy-start.30
  153.0 1.8 copy-start.35
  154.8 1.7 copy-start.31
  154.8 1.7 copy-start.17
  161.5 3.0 copy-start.13
  164.5 2.0 copy-start.37
  164.5 2.4 copy-start.16
  166.9 2.4 copy-start.23
  277.0 3.2 %copy-start.2 = (bf16[4,1024,1024]{2,1,0:T(8,128)(2,1)}, bf16[4,1024,1024]{2,1,0:T(8,128)(2,1)S(1)}, u32[]{:S(2)}) copy-start(bf16[4,1024,1024]{2,1,0:T(8,128)(2,1)S(1)} %get-tuple-element.28) | copy-start | bytes 25165828
  292.4 7.5 %copy-start.4 = (bf16[2,16,40,1024]{3,2,1,0:T(8,128)(2,1)S(1)}, bf16[2,16,40,1024]{3,2,1,0:T(8,128)(2,1)}, u32[]{:S(2)}) copy-start(bf16[2,16,40,1024]{3,2,1,0:T(8,128)(2,1)} %copy-done.3) | copy-start | bytes 7864324
  292.4 7.5 %copy-start.53 = (bf16[2,16,40,704]{3,2,1,0:T(8,128)(2,1)S(1)}, bf16[2,16,40,704]{3,2,1,0:T(8,128)(2,1)}, u32[]{:S(2)}) copy-start(bf16[2,16,40,704]{3,2,1,0:T(8,128)(2,1)} %get-tuple-element.30) | copy-start | bytes 5406724
  299.9 5.0 %copy-start.51 = (bf16[2,16,40,1024]{3,2,1,0:T(8,128)(2,1)S(1)}, bf16[2,16,40,1024]{3,2,1,0:T(8,128)(2,1)}, u32[]{:S(2)}) copy-start(bf16[2,16,40,1024]{3,2,1,0:T(8,128)(2,1)} %get-tuple-element.32) | copy-start | bytes 7864324
  299.9 5.0 %copy-start.52 = (bf16[2,16,40,704]{3,2,1,0:T(8,128)(2,1)S(1)}, bf16[2,16,40,704]{3,2,1,0:T(8,128)(2,1)}, u32[]{:S(2)}) copy-start(bf16[2,16,40,704]{3,2,1,0:T(8,128)(2,1)} %get-tuple-element.31) | copy-start | bytes 5406724
  304.9 5.0 %copy-start.1 = (bf16[1024,1024]{1,0:T(8,128)(2,1)S(1)}, bf16[1024,1024]{1,0:T(8,128)(2,1)}, u32[]{:S(2)}) copy-start(bf16[1024,1024]{1,0:T(8,128)(2,1)} %param.22) | copy-start | bytes 6291460
  (22 other events, 23.2 us)

commit v3 on v2

--- a/solution.py
+++ b/solution.py
@@ -61,155 +61,189 @@
     return out
 
 
-def send_rows(me, rows, recv, send_sem, recv_sem):
-    copies = []
-    for k in range(1, me.n_expert):
-        to = (me.e + k) % me.n_expert
-        copies.append(
-            remote(
-                rows.at[to], recv.at[me.c, me.y * me.n_expert + me.e],
-                send_sem.at[k], recv_sem.at[k], me.at(e=to),
+class Spread:
+    def __init__(self, me, rows, recv, sems):
+        self.me, self.rows, self.recv = me, rows, recv
+        self.se, self.re, self.sy, self.ry, self.sc, self.rc = sems
+        self.came, self.along, self.crossed = {}, {}, {}
+
+    def send(self):
+        me = self.me
+        for k in range(1, me.n_expert):
+            to = (me.e + k) % me.n_expert
+            self.came[k] = remote(
+                self.rows.at[to], self.recv.at[me.c, me.y * me.n_expert + me.e],
+                self.se.at[k], self.re.at[k], me.at(e=to),
             )
-        )
-    recv[me.c, me.y * me.n_expert + me.e] = rows[me.e]
-    return copies
-
-
-def pass_on(me, recv, came, sy, ry, sc, rc):
-    along_y = []
-    for k in range(me.n_expert):
-        src = (me.e - k + me.n_expert) % me.n_expert
-        if k:
-            came[k - 1].wait_recv()
-        block = recv.at[me.c, me.y * me.n_expert + src]
-        for s in range(1, me.ny):
-            along_y.append(
-                remote(block, block, sy.at[s - 1, k], ry.at[s - 1, k], me.at(y=(me.y + s) % me.ny))
-            )
-    block = recv.at[me.c, pl.ds(me.y * me.n_expert, me.n_expert)]
-    across = [remote(block, block, sc.at[0], rc.at[0], me.at(c=1 - me.c))]
-    return along_y, across
-
-
-def pass_across(me, recv, along_y, across, sc, rc):
-    for copy in along_y:
-        copy.wait_recv()
-    for s in range(1, me.ny):
-        column = (me.y - s + me.ny) % me.ny * me.n_expert
-        block = recv.at[me.c, pl.ds(column, me.n_expert)]
-        across.append(remote(block, block, sc.at[s], rc.at[s], me.at(c=1 - me.c)))
-
-
-def spread_kernel(
-    sizes, rows_per, info_ref, cot_ref, moe_ref, w_ref, g_out, x_out, w_out,
-    info_all, tok, wext, rows_g, rows_x, rows_w, sem_tok_s, sem_tok_r, se, re, sy, ry, sc, rc,
-):
-    me = Place(*sizes)
-    micro, cap, per_core = rows_per
-    seq = cot_ref.shape[0]
-    greet(column_peers(me))
-    mate = me.at(c=1 - me.c)
-    c = me.c
-    first = []
-    info_all[c] = info_ref[...]
-    tok[0, c] = cot_ref[...]
-    tok[1, c] = moe_ref[...]
-    lanes = lax.broadcasted_iota(jnp.int32, (seq, 128), 1)
-    for k in range(2):
-        w = w_ref[:, k : k + 1]
-        hi = w.astype(jnp.bfloat16).astype(jnp.float32)
-        mid = (w - hi).astype(jnp.bfloat16).astype(jnp.float32)
-        low = w - hi - mid
-        wext[c, k] = jnp.where(
-            lanes == 0, hi, jnp.where(lanes == 1, mid, jnp.where(lanes == 2, low, 0.0))
-        ).astype(jnp.bfloat16)
-    first.append(remote(info_all.at[c], info_all.at[c], sem_tok_s.at[0], sem_tok_r.at[0], mate))
-    first.append(remote(tok.at[0, c], tok.at[0, c], sem_tok_s.at[1], sem_tok_r.at[1], mate))
-    first.append(remote(tok.at[1, c], tok.at[1, c], sem_tok_s.at[2], sem_tok_r.at[2], mate))
-    first.append(remote(wext.at[c], wext.at[c], sem_tok_s.at[3], sem_tok_r.at[3], mate))
-    first[0].wait_recv()
-    n_rows = me.n_expert * 2 * per_core
-    row_ids = lax.broadcasted_iota(jnp.int32, (n_rows, seq), 0)
-    group = lax.broadcasted_iota(jnp.int32, (1, seq), 1) // (seq // micro)
-    hots = [[], []]
-    for cc in range(2):
+        self.recv[me.c, me.y * me.n_expert + me.e] = self.rows[me.e]
+
+    def pass_on(self, blocks):
+        me = self.me
+        for k in blocks:
+            if k:
+                self.came[k].wait_recv()
+            src = (me.e - k + me.n_expert) % me.n_expert
+            block = self.recv.at[me.c, me.y * me.n_expert + src]
+            for s in range(1, me.ny):
+                self.along[s, k] = remote(
+                    block, block, self.sy.at[s - 1, k], self.ry.at[s - 1, k], me.at(y=(me.y + s) % me.ny)
+                )
+
+    def cross(self, s):
+        me = self.me
+        if s:
+            for k in range(me.n_expert):
+                self.along[s, k].wait_recv()
+        block = self.recv.at[me.c, pl.ds((me.y - s + me.ny) % me.ny * me.n_expert, me.n_expert)]
+        self.crossed[s] = remote(block, block, self.sc.at[s], self.rc.at[s], me.at(c=1 - me.c))
+
+    def arrive(self):
+        for copy in self.crossed.values():
+            copy.wait_recv()
+
+    def close(self):
+        for copies in (self.came, self.along, self.crossed):
+            for copy in copies.values():
+                copy.wait_send()
+
+
+def spread_sems(sizes):
+    n_expert, ny = sizes[0], sizes[1] // 2
+    most = max(ny - 1, 1)
+    return [
+        DMA((3, n_expert)), DMA((3, n_expert)), DMA((3, most, n_expert)), DMA((3, most, n_expert)),
+        DMA((3, ny)), DMA((3, ny)),
+    ]
+
+
+class Rows:
+    def __init__(self, me, rows_per, info_ref, moe_ref, cot_ref, w_ref, info_all, tok, wext, send, recv):
+        self.me, self.rows_per, self.info_all, self.tok, self.wext = me, rows_per, info_all, tok, wext
+        seq = cot_ref.shape[0]
+        self.seq = seq
+        c, mate = me.c, me.at(c=1 - me.c)
+        info_all[c] = info_ref[...]
+        tok[0, c] = moe_ref[...]
+        lanes = lax.broadcasted_iota(jnp.int32, (seq, 128), 1)
         for k in range(2):
-            route = info_all[cc, k : k + 1, :]
-            slot = info_all[cc, 2 + k : 3 + k, :]
-            target = (route // 2) * (2 * per_core) + cc * per_core + group * cap + slot
-            target = jnp.where((slot >= 0) & (route % 2 == c), target, -1)
-            hots[k].append(jnp.where(row_ids == target, 1.0, 0.0))
-    hot1 = [h.astype(jnp.bfloat16) for h in hots[0]]
-    hot2 = [h.astype(jnp.bfloat16) for h in hots[1]]
-    both = [(p + q).astype(jnp.bfloat16) for p, q in zip(*hots)]
-
-    def gather(left, right):
+            w = w_ref[:, k : k + 1]
+            hi = w.astype(jnp.bfloat16).astype(jnp.float32)
+            mid = (w - hi).astype(jnp.bfloat16).astype(jnp.float32)
+            low = w - hi - mid
+            wext[c, k] = jnp.where(
+                lanes == 0, hi, jnp.where(lanes == 1, mid, jnp.where(lanes == 2, low, 0.0))
+            ).astype(jnp.bfloat16)
+        self.copies = [
+            remote(ref, ref, send.at[i], recv.at[i], mate)
+            for i, ref in enumerate((info_all.at[c], tok.at[0, c], wext.at[c]))
+        ]
+        tok[1, c] = cot_ref[...]
+        self.copies.append(remote(tok.at[1, c], tok.at[1, c], send.at[3], recv.at[3], mate))
+
+    def hots(self):
+        me, seq = self.me, self.seq
+        micro, cap, per_core = self.rows_per
+        self.copies[0].wait_recv()
+        row_ids = lax.broadcasted_iota(jnp.int32, (me.n_expert * 2 * per_core, seq), 0)
+        group = lax.broadcasted_iota(jnp.int32, (1, seq), 1) // (seq // micro)
+        hots = [[], []]
+        for cc in range(2):
+            for k in range(2):
+                route = self.info_all[cc, k : k + 1, :]
+                slot = self.info_all[cc, 2 + k : 3 + k, :]
+                target = (route // 2) * (2 * per_core) + cc * per_core + group * cap + slot
+                target = jnp.where((slot >= 0) & (route % 2 == me.c), target, -1)
+                hots[k].append(jnp.where(row_ids == target, 1.0, 0.0))
+        self.each = [[h.astype(jnp.bfloat16) for h in hots[k]] for k in range(2)]
+        self.both = [(p + q).astype(jnp.bfloat16) for p, q in zip(*hots)]
+
+    def gather(self, left, right):
         total = None
         for p, q in zip(left, right):
             term = jnp.dot(p, q, preferred_element_type=jnp.float32)
             total = term if total is None else total + term
-        return total.astype(jnp.bfloat16).reshape(me.n_expert, 2 * per_core, -1)
-
-    first[1].wait_recv()
-    rows_g[...] = gather(both, [tok[0, 0], tok[0, 1]])
-    came_g = send_rows(me, rows_g, g_out, se.at[0], re.at[0])
-    first[2].wait_recv()
-    first[3].wait_recv()
-    rows_x[...] = gather(both, [tok[1, 0], tok[1, 1]])
-    came_x = send_rows(me, rows_x, x_out, se.at[1], re.at[1])
-    rows_w[...] = gather(hot1 + hot2, [wext[0, 0], wext[1, 0], wext[0, 1], wext[1, 1]])
-    came_w = send_rows(me, rows_w, w_out, se.at[2], re.at[2])
-    state = []
-    for i, (ref, came) in enumerate(((g_out, came_g), (x_out, came_x), (w_out, came_w))):
-        state.append(pass_on(me, ref, came, sy.at[i], ry.at[i], sc.at[i], rc.at[i]))
-    for i, ref in enumerate((g_out, x_out, w_out)):
-        pass_across(me, ref, state[i][0], state[i][1], sc.at[i], rc.at[i])
-    for along_y, across in state:
-        for copy in across:
-            copy.wait()
-        for copy in along_y:
+        per_core = self.rows_per[2]
+        return total.astype(jnp.bfloat16).reshape(self.me.n_expert, 2 * per_core, -1)
+
+    def moe(self):
+        self.copies[1].wait_recv()
+        return self.gather(self.both, [self.tok[0, 0], self.tok[0, 1]])
+
+    def weights(self):
+        self.copies[2].wait_recv()
+        wext = self.wext
+        return self.gather(self.each[0] + self.each[1], [wext[0, 0], wext[1, 0], wext[0, 1], wext[1, 1]])
+
+    def cot(self):
+        self.copies[3].wait_recv()
+        return self.gather(self.both, [self.tok[1, 0], self.tok[1, 1]])
+
+    def close(self):
+        for copy in self.copies:
             copy.wait_send()
-    for copy in first + came_g + came_x + came_w:
-        copy.wait_send()
-
-
-def spread(sizes, micro, cap, info, cot, moe, weights):
-    n_expert, n_dp = sizes
-    ny, per_core = n_dp // 2, micro * cap
+
+
+def rows_scratch(sizes, per_core, seq, width):
+    mine = (sizes[0], 2 * per_core)
+    bf = jnp.bfloat16
+    return [
+        pltpu.VMEM((2, 8, seq), jnp.int32),
+        pltpu.VMEM((2, 2, seq, width), bf),
+        pltpu.VMEM((2, 2, seq, 128), bf),
+        DMA((4,)),
+        DMA((4,)),
+        pltpu.VMEM(mine + (width,), bf),
+        pltpu.VMEM(mine + (128,), bf),
+        pltpu.VMEM(mine + (width,), bf),
+    ]
+
+
+def send_out(me, rows_per, refs, recvs, scratch, sems):
+    rows = Rows(me, rows_per, *refs, *scratch[:5])
+    rows.hots()
+    out = []
+    for i, (make, buf) in enumerate(zip((rows.moe, rows.weights, rows.cot), scratch[5:])):
+        buf[...] = make()
+        payload = Spread(me, buf, recvs[i], [s.at[i] for s in sems])
+        payload.send()
+        out.append(payload)
+    return rows, out
+
+
+def spread_kernel(sizes, rows_per, info_ref, moe_ref, cot_ref, w_ref, x_out, w_out, g_out, *scratch):
+    me = Place(*sizes)
+    greet(column_peers(me))
+    rows, payloads = send_out(
+        me, rows_per, (info_ref, moe_ref, cot_ref, w_ref), (x_out, w_out, g_out), scratch[:8], scratch[8:]
+    )
+    for payload in payloads:
+        payload.pass_on(range(me.n_expert))
+        payload.cross(0)
+    for payload in payloads:
+        for s in range(1, me.ny):
+            payload.cross(s)
+    for payload in payloads:
+        payload.arrive()
+        payload.close()
+    rows.close()
+
+
+def spread(sizes, micro, cap, info, moe, cot, weights):
+    n_expert, ny, per_core = sizes[0], sizes[1] // 2, micro * cap
     seq, width = cot.shape
     block = (2, ny * n_expert, 2 * per_core)
-    mine = (n_expert, 2 * per_core)
     bf = jnp.bfloat16
     return pl.pallas_call(
         functools.partial(spread_kernel, sizes, (micro, cap, per_core)),
-        out_shape=(
-            jax.ShapeDtypeStruct(block + (width,), bf),
-            jax.ShapeDtypeStruct(block + (width,), bf),
-            jax.ShapeDtypeStruct(block + (128,), bf),
-        ),
+        out_shape=tuple(jax.ShapeDtypeStruct(block + (n,), bf) for n in (width, 128, width)),
         in_specs=[VMEM] * 4,
         out_specs=(VMEM,) * 3,
-        scratch_shapes=[
-            pltpu.VMEM((2,) + info.shape, jnp.int32),
-            pltpu.VMEM((2, 2, seq, width), bf),
-            pltpu.VMEM((2, 2, seq, 128), bf),
-            pltpu.VMEM(mine + (width,), bf),
-            pltpu.VMEM(mine + (width,), bf),
-            pltpu.VMEM(mine + (128,), bf),
-            DMA((4,)),
-            DMA((4,)),
-            DMA((3, n_expert)),
-            DMA((3, n_expert)),
-            DMA((3, ny, n_expert)),
-            DMA((3, ny, n_expert)),
-            DMA((3, ny)),
-            DMA((3, ny)),
-        ],
+        scratch_shapes=rows_scratch(sizes, per_core, seq, width) + spread_sems(sizes),
         name="spread",
         compiler_params=pltpu.CompilerParams(
             collective_id=1, has_side_effects=True, vmem_limit_bytes=48 << 20
         ),
-    )(info, cot, moe, weights)
+    )(info, moe, cot, weights)
 
 
 class Back:
@@ -338,9 +372,9 @@
 
 
 def expert_kernel(
-    sizes, x_ref, g_ref, w_ref, wg_hbm, wu_hbm, wd_hbm,
-    q_out, hid_out, dg_out, du_out, gr_out,
-    wg, wu, wd, act, slope, away, own, sem_w, *scratch,
+    sizes, rows_per, info_ref, moe_ref, cot_ref, w_in, wg_hbm, wu_hbm, wd_hbm,
+    q_out, x_ref, hid_out, dg_out, du_out, gr_out,
+    g_ref, w_ref, wg, wu, wd, act, slope, away, own, sem_w, *scratch,
 ):
     me = Place(*sizes)
     c = me.c
@@ -350,6 +384,10 @@
             fetch[n, i] = pltpu.make_async_copy(src.at[j], dst.at[j], sem_w.at[n, i])
             fetch[n, i].start()
     greet(column_peers(me))
+    rows_of, (out_x, out_w, out_g) = send_out(
+        me, rows_per, (info_ref, moe_ref, cot_ref, w_in), (x_ref, w_ref, g_ref), scratch[:8], scratch[8:14]
+    )
+    scratch = scratch[14:]
     bf, f32 = jnp.bfloat16, jnp.float32
     size = x_ref.shape[2]
     column = me.n_expert
@@ -386,8 +424,8 @@
     def forward(first, j, start, count):
         def body(some, rows):
             x = flat(x_ref[j, some])
-            gate_pre = dot(x, wg[j], ((1,), (0,)))
-            up_pre = dot(x, wu[j], ((1,), (0,)))
+            gate_pre = dot(x, wg[j], ((1,), (1,)))
+            up_pre = dot(x, wu[j], ((1,), (1,)))
             hidden, active, lean = gated_terms(gate_pre, up_pre)
             act[j, rows, :] = active
             slope[j, rows, :] = lean
@@ -408,20 +446,34 @@
             du = (grad_hidden * act[j, rows, :]).astype(bf)
             dg_out[j, some] = blocks(dg)
             du_out[j, some] = blocks(du)
-            store(1, first, some, rows, dot(dg, wg[j], ((1,), (1,))) + dot(du, wu[j], ((1,), (1,))))
+            store(1, first, some, rows, dot(dg, wg[j], ((1,), (0,))) + dot(du, wu[j], ((1,), (0,))))
 
         each(start, count, body)
 
+    for payload in (out_x, out_w):
+        payload.pass_on(range(column))
+        payload.cross(0)
+    for payload in (out_x, out_w):
+        for s in range(1, me.ny):
+            payload.cross(s)
     for i in range(3):
         fetch[0, i].wait()
+    out_x.arrive()
     forward(True, 1 - c, 0, me.ny * column)
     back.to_mate(0)
+    out_g.pass_on(range(half))
     for i in range(3):
         fetch[1, i].wait()
     for k in range(1, me.ny):
         forward(False, c, back.ys[k] * column, column)
     back.along_y(0)
+    out_g.pass_on(range(half, column))
+    out_g.cross(0)
     forward(False, c, me.y * column, column)
+    for s in range(1, me.ny):
+        out_g.cross(s)
+    out_g.arrive()
+    out_w.arrive()
     backward(True, 1 - c, 0, me.ny * column)
     back.to_mate(1)
     back.finish(0, back.order[:half])
@@ -434,25 +486,30 @@
     back.finish(1, back.order)
     back.across(1)
     back.close()
-
-
-def experts(sizes, x, g, w, w_gate, w_up, w_down):
-    n_expert = sizes[0]
-    _, count, size, width = x.shape
-    units = w_gate.shape[2]
+    for payload in (out_x, out_w, out_g):
+        payload.close()
+    rows_of.close()
+
+
+def experts(sizes, micro, cap, info, moe, cot, weights, w_gate, w_up, w_down):
+    n_expert, ny, per_core = sizes[0], sizes[1] // 2, micro * cap
+    seq, width = cot.shape
+    units = w_down.shape[1]
+    count, size = ny * n_expert, 2 * per_core
     bf, f32 = jnp.bfloat16, jnp.float32
     any_space = pl.BlockSpec(memory_space=pl.ANY)
     inner = jax.ShapeDtypeStruct((2, count, size, units), bf)
+    outer = jax.ShapeDtypeStruct((2, count, size, width), bf)
     return pl.pallas_call(
-        functools.partial(expert_kernel, sizes),
+        functools.partial(expert_kernel, sizes, (micro, cap, per_core)),
         out_shape=(
-            jax.ShapeDtypeStruct((2, 2, n_expert, size, width), bf),
-            inner, inner, inner,
-            jax.ShapeDtypeStruct(x.shape, bf),
+            jax.ShapeDtypeStruct((2, 2, n_expert, size, width), bf), outer, inner, inner, inner, outer,
         ),
-        in_specs=[VMEM] * 3 + [any_space] * 3,
-        out_specs=(VMEM,) * 5,
+        in_specs=[VMEM] * 4 + [any_space] * 3,
+        out_specs=(VMEM,) * 6,
         scratch_shapes=[
+            pltpu.VMEM((2, count, size, width), bf),
+            pltpu.VMEM((2, count, size, 128), bf),
             pltpu.VMEM(w_gate.shape, bf),
             pltpu.VMEM(w_up.shape, bf),
             pltpu.VMEM(w_down.shape, bf),
@@ -462,12 +519,83 @@
             pltpu.VMEM((2, count * size, width), f32),
             DMA((2, 3)),
         ]
+        + rows_scratch(sizes, per_core, seq, width)
+        + spread_sems(sizes)
         + back_scratch(sizes, size, width),
         name="experts",
         compiler_params=pltpu.CompilerParams(
             collective_id=4, has_side_effects=True, vmem_limit_bytes=60 << 20
         ),
-    )(x, g, w, w_gate, w_up, w_down)
+    )(info, moe, cot, weights, w_gate, w_up, w_down)
+
+
+def finish_kernel(sums_ref, x_hbm, h_hbm, dg_hbm, du_hbm, gr_hbm, *refs):
+    outs, (x, h, dg, du, gr, stage, sem_in, sem_out) = refs[:7], refs[7:]
+    loads = []
+    for i, (src, dst) in enumerate(((x_hbm, x), (h_hbm, h), (dg_hbm, dg), (du_hbm, du), (gr_hbm, gr))):
+        loads.append(pltpu.make_async_copy(src, dst, sem_in.at[i]))
+        loads[-1].start()
+    slots, rows = stage.shape[:2]
+    width = sums_ref.shape[1]
+    units = h.shape[2]
+    jobs = []
+    products = [
+        (left, right, out, j, f)
+        for left, right, out in ((dg, x, outs[4]), (du, x, outs[5]), (h, gr, outs[6]))
+        for j in range(2)
+        for f in range(0, units, rows)
+    ]
+    casts = [(m, r) for m in range(4) for r in range(0, width, rows)]
+    while casts or products:
+        if casts:
+            jobs.append(casts.pop(0))
+        if products and (len(jobs) > 3 or not casts):
+            jobs.append(products.pop(0))
+    flying = [None] * slots
+    loaded = False
+    for n, job in enumerate(jobs):
+        slot = n % slots
+        if flying[slot] is not None:
+            flying[slot].wait()
+        if len(job) == 2:
+            m, r = job
+            stage[slot] = sums_ref[m, r : r + rows, :].astype(jnp.float32)
+            src, dst = stage.at[slot], outs[m].at[pl.ds(r, rows)]
+        else:
+            if not loaded:
+                for load in loads:
+                    load.wait()
+                loaded = True
+            left, right, out, j, f = job
+            size = min(rows, units - f)
+            stage[slot, :size] = lax.dot_general(
+                left[j, :, f : f + size], right[j], (((0,), (0,)), ((), ())),
+                preferred_element_type=jnp.float32,
+            )
+            src, dst = stage.at[slot, pl.ds(0, size)], out.at[j, pl.ds(f, size)]
+        flying[slot] = pltpu.make_async_copy(src, dst, sem_out.at[slot])
+        flying[slot].start()
+    for copy in flying:
+        if copy is not None:
+            copy.wait()
+
+
+def finish(sums, x, h, dg, du, gr):
+    f32 = jnp.float32
+    width = sums.shape[1]
+    units = h.shape[2]
+    any_space = pl.BlockSpec(memory_space=pl.ANY)
+    return pl.pallas_call(
+        finish_kernel,
+        out_shape=(jax.ShapeDtypeStruct((width, width), f32),) * 4
+        + (jax.ShapeDtypeStruct((2, units, width), f32),) * 3,
+        in_specs=[VMEM] + [any_space] * 5,
+        out_specs=(any_space,) * 7,
+        scratch_shapes=[pltpu.VMEM(a.shape, a.dtype) for a in (x, h, dg, du, gr)]
+        + [pltpu.VMEM((4, 256, width), f32), DMA((5,)), DMA((4,))],
+        name="finish",
+        compiler_params=pltpu.CompilerParams(vmem_limit_bytes=32 << 20),
+    )(sums, x, h, dg, du, gr)
 
 
 def reduce_kernel(
@@ -797,14 +925,16 @@
     weights = jnp.concatenate([weight_first, weight_second], axis=1)
 
     info = jnp.concatenate([routes.T, queue_slots.T, jnp.zeros((4, seq_len), jnp.int32)])
-    grad_in, rows_in, weight_in = spread(
-        sizes, MICRO, capacity, info, cotangent, moe_in.astype(bf), weights
-    )
-    if 23 * rows_in.size + 6 * w_gate.size < 52 << 20:
-        back, hidden, gate_grad, up_grad, grad_rows = experts(
-            sizes, rows_in, grad_in, weight_in, w_gate, w_up, w_down
+    gate_t, up_t = jnp.swapaxes(w_gate, 1, 2), jnp.swapaxes(w_up, 1, 2)
+    slots = n_dp // 2 * n_expert * 2 * MICRO * capacity
+    if 2 * slots * width * 20 + 6 * w_gate.size < 52 << 20:
+        back, rows_in, hidden, gate_grad, up_grad, grad_rows = experts(
+            sizes, MICRO, capacity, info, moe_in.astype(bf), cotangent, weights, gate_t, up_t, w_down
         )
     else:
+        rows_in, weight_in, grad_in = spread(
+            sizes, MICRO, capacity, info, moe_in.astype(bf), cotangent, weights
+        )
         blocks = rows_in.shape[:-1] + (-1,)
         rows_in, grad_in, weight_in = [
             a.reshape(2, -1, a.shape[-1]) for a in (rows_in, grad_in, weight_in)
@@ -823,9 +953,6 @@
     rows_in, hidden, gate_grad, up_grad, grad_rows = [
         a.reshape(2, -1, a.shape[-1]) for a in (rows_in, hidden, gate_grad, up_grad, grad_rows)
     ]
-    grad_w_gate = dot32("jrd,jrf->jdf", rows_in, gate_grad)
-    grad_w_up = dot32("jrd,jrf->jdf", rows_in, up_grad)
-    grad_w_down = dot32("jrf,jrd->jfd", hidden, grad_rows)
     back = back.reshape(2, -1, width)
 
     core = lax.axis_index("dp") % 2
@@ -890,7 +1017,10 @@
         jnp.stack([grad_queries, grad_keys, grad_values, grad_attn_low]),
         small,
     )
-    matrices = [sums[i].astype(f32) for i in range(4)]
+    *matrices, grad_w_gate, grad_w_up, grad_w_down = finish(
+        sums, rows_in, hidden, gate_grad, up_grad, grad_rows
+    )
+    grad_w_gate, grad_w_up = jnp.swapaxes(grad_w_gate, 1, 2), jnp.swapaxes(grad_w_up, 1, 2)
     return (
         layer_out, grad_input, small[expert_count], *matrices,
         small[expert_count + 2, : table.size].reshape(buckets, heads),

time: 311 us -> 301 us (0.968)
  Pallas kernels: 209 us -> 232 us
  matrix products: 47.5 us -> 27.8 us
  other arithmetic: 17.3 us -> 8.39 us
  local copies, waits for them, and re-layouts: 34.9 us -> 30.7 us
    pallas_call x2, Pallas kernels: 108 us -> 133 us  [the longest x1 117 us: experts(): pl.pallas_call(functools.partial(expert_kernel, sizes, (micro, cap, per_c...]
    dot_general x20 -> x17, matrix products: 41.7 us -> 23.5 us  [dot32(): return jnp.einsum(pattern, left, right, preferred_element_type=jnp.float32)]
    convert_element_type x1 -> x0, other arithmetic: 10.2 us -> none  [shards(): matrices = [sums[i].astype(f32) for i in range(4)]]
    unnamed x111 -> x81, local copies, waits for them, and re-layouts: 21.3 us -> 17 us
where the time goes in v3:
time: 301 us
  Pallas kernels  232 us (77%)
  local copies, waits for them, and re-layouts  30.7 us (10%)
  matrix products  27.8 us (9%)
  other arithmetic  8.39 us (3%)
    pallas_call x1, Pallas kernels, experts(): pl.pallas_call(functools.partial(expert_kernel, sizes, (micro, cap, per_c...  117 us
    pallas_call x1, Pallas kernels, reduce_all(): pl.pallas_call(functools.partial(reduce_kernel, sizes, pieces), out_shape...  99.7 us
    dot_general x17, matrix products, dot32(): return jnp.einsum(pattern, left, right, preferred_element_type=jnp.float32)  23.5 us
    unnamed x81, local copies, waits for them, and re-layouts  17 us
    pallas_call x1, Pallas kernels, finish(): pl.pallas_call(finish_kernel, out_shape=(jax.ShapeDtypeStruct((width, wid...  15.6 us

profile of v3, /device:TPU:1, one launch (start us, length us, event | category | flops | bytes accessed | tf_op | source)
XLA Modules:
  0.0 300.6 jit_solution(8938064248544392248)
XLA Ops:
  0.7 1.2 fusion.18
  3.3 1.3 slice_bitcast_fusion.3
  4.6 1.4 add_add_fusion.info_ref
  6.0 2.2 convolution_convert_fusion.5
  9.1 2.1 convolution_convert_fusion.6
  12.0 2.1 convolution_convert_fusion.7
  15.7 1.4 copy.74
  17.1 1.7 convolution_add_fusion
  18.9 1.3 fusion.82
  20.2 2.0 convolution_convert_fusion.4
  22.2 1.8 copy.81
  24.0 1.5 multiply_reduce_fusion.3
  27.9 117.1 %experts.1 = (bf16[2,2,8,40,1024]{4,3,2,1,0:T(8,128)(2,1)}, bf16[2,16,40,1024]{3,2,1,0:T(8,128)(2,1)}, bf16[2,16,40,704]{3,2,1,0:T(8,128)(2,1)}, bf16[2,16,40,70...) custom-call(s32[8,128]{1,0:T(8,128)} %add_add_fusion.info_ref, ...), custom_call_target="tpu_custom_call" | custom-call | tf_op jit(solution)/shard_map/experts/pallas_call | solution.py:503
  145.0 2.0 fusion.80
  148.1 1.1 fusion.21
  149.8 1.2 multiply_reduce_fusion.1
  151.1 1.0 convert_bitcast_fusion
  153.1 2.1 convolution_convert_fusion
  157.5 1.2 convolution_convert_fusion.1
  158.6 1.0 convolution_convert_fusion.2
  160.2 1.2 fusion.5
  161.9 2.5 fusion.84
  167.3 1.0 fusion.16
  168.4 99.7 %reduce_all.1 = (bf16[4,1024,1024]{2,1,0:T(8,128)(2,1)S(1)}, f32[32,1024]{1,0:T(8,128)S(1)}) custom-call(bf16[2,128,1024]{2,1,0:T(8,128)(2,1)S(1)} %pad_maximum_fusion.1.left_ref, bf16[4,128,1024]{2,1,0:T(8,128)(2,1)S(1)} %pad_maximum_fusion.right_ref, f32[32,1024]{1,0:T(8,128)S(1)} %select_maximum_fusion.small_ref), custom_call_target="tpu_custom_call" | custom-call | tf_op jit(solution)/shard_map/reduce_all/pallas_call | solution.py:826
  268.1 3.2 %copy-done.2 = bf16[4,1024,1024]{2,1,0:T(8,128)(2,1)} copy-done((bf16[4,1024,1024]{2,1,0:T(8,128)(2,1)}, bf16[4,1024,1024]{2,1,0:T(8,128)(2,1)S(1)}, u32[]{:S(2)}) %copy-start.2) | copy-done | bytes 8388632
  273.3 3.4 %copy-done.3 = bf16[4,1024,1024]{2,1,0:T(8,128)(2,1)S(1)} copy-done((bf16[4,1024,1024]{2,1,0:T(8,128)(2,1)S(1)}, bf16[4,1024,1024]{2,1,0:T(8,128)(2,1)}, u32[]{:S(2)}) %copy-start.3) | copy-done | bytes 8388632
  276.7 1.7 copy-done.4
  278.4 1.7 copy-done.5
  280.2 1.5 copy-done.6
  281.7 1.5 copy-done.7
  283.2 1.5 copy-done.8
  284.8 15.6 %finish.1 = (f32[1024,1024]{1,0:T(8,128)}, f32[1024,1024]{1,0:T(8,128)}, f32[1024,1024]{1,0:T(8,128)}, f32[1024,1024]{1,0:T(8,128)}, f32[2,704,1024]{2,1,0:T(8,1...) custom-call(bf16[4,1024,1024]{2,1,0:T(8,128)(2,1)S(1)} %copy-done.3, bf16[2,640,1024]{2,1,0:T(8,128)(2,1)S(1)} %bitcast.98, ...), custom_call_target="tpu_custom_call" | custom-call | tf_op jit(solution)/shard_map/finish/pallas_call | solution.py:588
  (120 shorter events, 17.7 us)
Async XLA Ops:
  0.6 23.4 %copy-start = (bf16[1024,1024]{1,0:T(8,128)(2,1)S(1)}, bf16[1024,1024]{1,0:T(8,128)(2,1)}, u32[]{:S(2)}) copy-start(bf16[1024,1024]{1,0:T(8,128)(2,1)} %param.22) | copy-start | bytes 6291460
  0.7 8.4 %copy-start.9 = (bf16[128,1024]{1,0:T(8,128)(2,1)S(1)}, bf16[128,1024]{1,0:T(8,128)(2,1)}, u32[]{:S(2)}) copy-start(bf16[128,1024]{1,0:T(8,128)(2,1)} %param.15) | copy-start | bytes 786436
  0.7 8.4 %copy-start.28 = (f32[1024]{0:T(1024)S(1)}, f32[1024]{0:T(1024)}, u32[]{:S(2)}) copy-start(f32[1024]{0:T(1024)} %param.18) | copy-start | bytes 12292
  1.9 10.1 %copy-start.31 = (f32[128]{0:T(128)}, f32[128]{0:T(128)S(1)}, u32[]{:S(2)}) copy-start(f32[128]{0:T(128)S(1)} %add_rsqrt_fusion.1) | copy-start | bytes 1540
  11.2 3.8 %copy-start.33 = (f32[32,16]{0,1:T(8,128)S(1)}, f32[32,16]{0,1:T(8,128)}, u32[]{:S(2)}) copy-start(f32[32,16]{0,1:T(8,128)} %param.23) | copy-start | bytes 6148
  18.9 3.4 %copy-start.13 = (f32[16,128,128]{1,2,0:T(8,128)}, f32[16,128,128]{1,2,0:T(8,128)S(1)}, u32[]{:S(2)}) copy-start(f32[16,128,128]{1,2,0:T(8,128)S(1)} %convolution_add_fusion) | copy-start | bytes 3145732
  22.2 3.4 %copy-start.24 = (f32[1024,16]{0,1:T(8,128)S(1)}, f32[1024,16]{0,1:T(8,128)}, u32[]{:S(2)}) copy-start(f32[1024,16]{0,1:T(8,128)} %param.25) | copy-start | bytes 196612
  22.2 3.4 %copy-start.27 = (f32[1024]{0:T(1024)S(1)}, f32[1024]{0:T(1024)}, u32[]{:S(2)}) copy-start(f32[1024]{0:T(1024)} %param.24) | copy-start | bytes 12292
  24.0 2.2 copy-start.34
  24.0 2.2 copy-start.36
  25.6 122.5 %copy-start.29 = (f32[128]{0:T(128)}, f32[128]{0:T(128)S(1)}, u32[]{:S(2)}) copy-start(f32[128]{0:T(128)S(1)} %add_rsqrt_fusion) | copy-start | bytes 1540
  145.0 2.1 copy-start.39
  145.0 2.5 copy-start.16
  145.0 2.5 copy-start.38
  147.1 2.1 copy-start.35
  147.1 2.1 copy-start.37
  149.2 1.9 copy-start.30
  153.1 3.0 %copy-start.12 = (f32[16,128,128]{1,2,0:T(8,128)S(1)}, f32[16,128,128]{1,2,0:T(8,128)}, u32[]{:S(2)}) copy-start(f32[16,128,128]{1,2,0:T(8,128)} %get-tuple-element.108) | copy-start | bytes 3145732
  153.1 3.0 %copy-start.25 = (bf16[128,1024]{0,1:T(8,128)(2,1)S(1)}, bf16[128,1024]{0,1:T(8,128)(2,1)}, u32[]{:S(2)}) copy-start(bf16[128,1024]{0,1:T(8,128)(2,1)} %copy.71) | copy-start | bytes 786436
  156.5 2.1 copy-start.14
  158.6 2.8 copy-start.17
  159.6 2.0 copy-start.18
  160.1 1.6 copy-start.20
  160.2 1.6 copy-start.23
  161.8 2.7 copy-start.10
  164.5 1.6 copy-start.11
  164.5 1.6 copy-start.22
  268.1 3.2 %copy-start.2 = (bf16[4,1024,1024]{2,1,0:T(8,128)(2,1)}, bf16[4,1024,1024]{2,1,0:T(8,128)(2,1)S(1)}, u32[]{:S(2)}) copy-start(bf16[4,1024,1024]{2,1,0:T(8,128)(2,1)S(1)} %get-tuple-element.30.sums_ref) | copy-start | bytes 25165828
  273.3 3.4 %copy-start.3 = (bf16[4,1024,1024]{2,1,0:T(8,128)(2,1)S(1)}, bf16[4,1024,1024]{2,1,0:T(8,128)(2,1)}, u32[]{:S(2)}) copy-start(bf16[4,1024,1024]{2,1,0:T(8,128)(2,1)} %copy-done.2) | copy-start | bytes 25165828
  276.7 1.7 copy-start.4
  278.4 1.7 copy-start.5
  284.8 15.6 %copy-start.1 = (bf16[1024,1024]{1,0:T(8,128)(2,1)S(1)}, bf16[1024,1024]{1,0:T(8,128)(2,1)}, u32[]{:S(2)}) copy-start(bf16[1024,1024]{1,0:T(8,128)(2,1)} %param.22) | copy-start | bytes 6291460
  (8 other events, 10.4 us)
